TPU v7x, 32 devices: a whole 2x2x4 slice. The times are simulated.
32 devices in a mesh: dp: 4 (over x, core), ctx: 8 (over z, y).
Axes of the slice: x: 2, y: 2, z: 4, core: 2. Of those that a mesh axis runs over, the one named last changes fastest.
Arguments:
- tokens: bfloat16 [4, 4096, 512], P('dp', 'ctx'), may hold values from -6 to 6
- piece_starts: int32 [4, 4], P('dp'), may hold values from 0 to 3840, as said below
- qkv_weight: bfloat16 [786432], P(('dp', 'ctx')), may hold values from -0.375 to 0.375
- out_weight: bfloat16 [262144], P(('dp', 'ctx')), may hold values from -0.75 to 0.75
- up_weight: bfloat16 [1048576], P(('dp', 'ctx')), may hold values from -0.25 to 0.25
- down_weight: bfloat16 [1048576], P(('dp', 'ctx')), may hold values from -0.125 to 0.125
- biases: bfloat16 [4096], P(('dp', 'ctx')), may hold values from -2 to 2
- norms: bfloat16 [2048], P(('dp', 'ctx'))
- cotangent: bfloat16 [4, 4096, 512], P('dp', 'ctx'), may hold values from -6 to 6
Outputs:
- output: bfloat16 [4, 4096, 512], P('dp', 'ctx')
- grad_tokens: float32 [4, 4096, 512], P('dp', 'ctx')
- grad_qkv: float32 [786432], P(('dp', 'ctx'))
- grad_out: float32 [262144], P(('dp', 'ctx'))
- grad_up: float32 [1048576], P(('dp', 'ctx'))
- grad_down: float32 [1048576], P(('dp', 'ctx'))
- grad_biases: float32 [4096], P(('dp', 'ctx'))
- grad_norms: float32 [2048], P(('dp', 'ctx'))
Inputs may be any that keep to these rules, and one draw needn't show every extreme that they name: `piece_starts`: each row holds 4 distinct multiples of 256 in increasing order; the first is 0 and the last 3840, so that every sequence opens and closes with a picture piece; a piece covers the 256 words from its start.
All inputs are finite; a program needn't handle non-finite values.
Results may differ from a plain program's by a relative error of at most 0.02.
Values may be sent and summed in bfloat16 or wider, within the bound.
A program may use at most 256 MiB of HBM per device.

v0:
```python
import jax
import jax.numpy as jnp
from jax import lax
from jax.sharding import PartitionSpec as P

HEADS = 8
PIECE = 256


eps_norm = 1e-05
masked_score = -1e30


def layer_norm(values, gain, shift):
    center = jnp.mean(values, axis=-1, keepdims=True)
    offsets = values - center
    spread = jnp.mean(offsets * offsets, axis=-1, keepdims=True)
    return offsets * lax.rsqrt(spread + eps_norm) * gain + shift


def gelu_exact(values):
    return jax.nn.gelu(values, approximate=False)


def piece_flags(positions, starts_row):
    opening = positions // PIECE * PIECE
    return jnp.any(opening[:, None] == starts_row[None, :], axis=1)


def visible(query_pos, query_flag, key_pos):
    causal = key_pos[None, :] <= query_pos[:, None]
    same_piece = key_pos[None, :] // PIECE == query_pos[:, None] // PIECE
    return jnp.logical_or(causal, jnp.logical_and(same_piece, query_flag[:, None]))


def to_blocks(arrays, shard_rows):
    block_len = 256
    block_count = shard_rows // block_len
    shaped = tuple((member.reshape(block_count, block_len, HEADS, -1) for member in arrays))
    return (block_len, block_count, shaped)


def keep_state(state):
    return state


def unpack(flats, model_width):
    qkv_flat, out_flat, up_flat, down_flat, bias_flat, norm_flat = flats
    hidden = up_flat.shape[0] // model_width
    return (
        qkv_flat.reshape(model_width, 3 * model_width),
        out_flat.reshape(model_width, model_width),
        up_flat.reshape(model_width, hidden),
        down_flat.reshape(hidden, model_width),
        bias_flat.astype(jnp.float32),
        norm_flat.astype(jnp.float32),
    )


def norm_back(values, gain, shift, upstream):
    _, pullback = jax.vjp(layer_norm, values, gain, shift)
    return pullback(upstream)


def column_sum(matrix):
    return jnp.sum(matrix.astype(jnp.float32), axis=0)


def query_terms(
    query_heads,
    grad_heads,
    own_lse,
    own_delta,
    query_pos,
    query_flag,
    key_block,
    value_block,
    key_pos,
    factor,
):
    scores = (
        jnp.einsum("qhd,khd->hqk", query_heads, key_block, preferred_element_type=jnp.float32)
        * factor
    )
    allowed = visible(query_pos, query_flag, key_pos)[None]
    softmax_p = jnp.where(allowed, jnp.exp(scores - own_lse[:, :, None]), 0.0)
    dprobs = jnp.einsum("qhd,khd->hqk", grad_heads, value_block, preferred_element_type=jnp.float32)
    dscores = (softmax_p * (dprobs - own_delta[:, :, None])).astype(jnp.bfloat16)
    return (
        jnp.einsum("hqk,khd->hqd", dscores, key_block, preferred_element_type=jnp.float32) * factor
    )


def key_terms(
    query_block,
    grad_block,
    lse_block,
    delta_block,
    remote_pos,
    remote_flag,
    key_heads,
    value_heads,
    key_pos,
    factor,
):
    scores = (
        jnp.einsum("qhd,khd->hqk", query_block, key_heads, preferred_element_type=jnp.float32)
        * factor
    )
    allowed = visible(remote_pos, remote_flag, key_pos)[None]
    softmax_p = jnp.where(allowed, jnp.exp(scores - lse_block[:, :, None]), 0.0)
    dprobs = jnp.einsum("qhd,khd->hqk", grad_block, value_heads, preferred_element_type=jnp.float32)
    dscores = (softmax_p * (dprobs - delta_block[:, :, None])).astype(jnp.bfloat16)
    grad_keys = (
        jnp.einsum("hqk,qhd->hkd", dscores, query_block, preferred_element_type=jnp.float32)
        * factor
    )
    grad_values = jnp.einsum(
        "hqk,qhd->hkd",
        softmax_p.astype(jnp.bfloat16),
        grad_block,
        preferred_element_type=jnp.float32,
    )
    return (grad_keys, grad_values)


def per_device(
    tokens, piece_starts, qkv_weight, out_weight, up_weight, down_weight, biases, norms, cotangent
):
    model_width = tokens.shape[2]
    seq_rows = tokens.shape[1]
    params = unpack(
        (
            lax.all_gather(qkv_weight, ("dp", "ctx"), axis=0, tiled=True),
            lax.all_gather(out_weight, ("dp", "ctx"), axis=0, tiled=True),
            lax.all_gather(up_weight, ("dp", "ctx"), axis=0, tiled=True),
            lax.all_gather(down_weight, ("dp", "ctx"), axis=0, tiled=True),
            lax.all_gather(biases, ("dp", "ctx"), axis=0, tiled=True),
            lax.all_gather(norms, ("dp", "ctx"), axis=0, tiled=True),
        ),
        model_width,
    )
    qkv_mat, out_mat, up_mat, down_mat, bias_all, norm_all = params
    hidden = up_mat.shape[1]
    head_dim = model_width // HEADS
    factor = head_dim ** (-0.5)
    first_row = lax.axis_index("ctx") * seq_rows
    last_row = first_row + seq_rows - 1
    query_pos = first_row + jnp.arange(seq_rows, dtype=jnp.int32)
    starts_row = piece_starts[0]
    query_flag = piece_flags(query_pos, starts_row)
    bias_q = bias_all[:model_width]
    bias_v = bias_all[model_width : 2 * model_width]
    bias_o = bias_all[2 * model_width : 3 * model_width]
    bias_up = bias_all[3 * model_width : 3 * model_width + hidden]
    bias_down = bias_all[3 * model_width + hidden :]
    gain_one = norm_all[:model_width]
    shift_one = norm_all[model_width : 2 * model_width]
    gain_two = norm_all[2 * model_width : 3 * model_width]
    shift_two = norm_all[3 * model_width :]
    inputs = tokens[0].astype(jnp.float32)
    first_in = layer_norm(inputs, gain_one, shift_one).astype(jnp.bfloat16)
    projected = jnp.dot(first_in, qkv_mat, preferred_element_type=jnp.float32)
    queries = (projected[:, :model_width] + bias_q).astype(jnp.bfloat16)
    key_rows = projected[:, model_width : 2 * model_width].astype(jnp.bfloat16)
    value_rows = (projected[:, 2 * model_width :] + bias_v).astype(jnp.bfloat16)
    query_heads = queries.reshape(seq_rows, HEADS, head_dim)
    key_heads = key_rows.reshape(seq_rows, HEADS, head_dim)
    value_heads = value_rows.reshape(seq_rows, HEADS, head_dim)
    start_state = (
        jnp.full((HEADS, seq_rows), masked_score, jnp.float32),
        jnp.zeros((HEADS, seq_rows), jnp.float32),
        jnp.zeros((HEADS, seq_rows, head_dim), jnp.float32),
    )
    shard = (
        lax.all_gather(key_rows, "ctx", axis=0, tiled=True),
        lax.all_gather(value_rows, "ctx", axis=0, tiled=True),
    )
    shard_rows = shard[0].shape[0]
    block_len, block_count, (key_blocks, value_blocks) = to_blocks(shard, shard_rows)

    def forward_one_block(state, block_in):
        running_max, running_sum, running_acc = state
        key_block, value_block, position = block_in
        key_pos = position * block_len + jnp.arange(block_len, dtype=jnp.int32)
        scores = (
            jnp.einsum("qhd,khd->hqk", query_heads, key_block, preferred_element_type=jnp.float32)
            * factor
        )
        allowed = visible(query_pos, query_flag, key_pos)[None]
        scores = jnp.where(allowed, scores, masked_score)
        new_max = jnp.maximum(running_max, jnp.max(scores, axis=-1))
        correction = jnp.exp(running_max - new_max)
        exp_scores = jnp.where(allowed, jnp.exp(scores - new_max[:, :, None]), 0.0)
        running_sum = running_sum * correction + jnp.sum(exp_scores, axis=-1)
        running_acc = running_acc * correction[:, :, None] + jnp.einsum(
            "hqk,khd->hqd",
            exp_scores.astype(jnp.bfloat16),
            value_block,
            preferred_element_type=jnp.float32,
        )
        return ((new_max, running_sum, running_acc), None)

    def forward_compute(state):
        return lax.scan(
            forward_one_block,
            state,
            (key_blocks, value_blocks, jnp.arange(block_count, dtype=jnp.int32)),
        )[0]

    run_max, run_sum, run_acc = lax.cond(
        jnp.int32(0) <= last_row, forward_compute, keep_state, start_state
    )
    mixed_heads = run_acc / run_sum[:, :, None]
    mixed_f = jnp.transpose(mixed_heads, (1, 0, 2)).reshape(seq_rows, model_width)
    mixed_b = mixed_f.astype(jnp.bfloat16)
    log_sum = run_max + jnp.log(run_sum)
    after_attn = inputs + jnp.dot(mixed_b, out_mat, preferred_element_type=jnp.float32) + bias_o
    second_in = layer_norm(after_attn, gain_two, shift_two).astype(jnp.bfloat16)
    pre_act = jnp.dot(second_in, up_mat, preferred_element_type=jnp.float32) + bias_up
    activated = gelu_exact(pre_act).astype(jnp.bfloat16)
    result = (
        after_attn + jnp.dot(activated, down_mat, preferred_element_type=jnp.float32) + bias_down
    )
    output = result.astype(jnp.bfloat16)[None]
    back = unpack(
        (
            lax.all_gather(qkv_weight, ("dp", "ctx"), axis=0, tiled=True),
            lax.all_gather(out_weight, ("dp", "ctx"), axis=0, tiled=True),
            lax.all_gather(up_weight, ("dp", "ctx"), axis=0, tiled=True),
            lax.all_gather(down_weight, ("dp", "ctx"), axis=0, tiled=True),
            lax.all_gather(biases, ("dp", "ctx"), axis=0, tiled=True),
            lax.all_gather(norms, ("dp", "ctx"), axis=0, tiled=True),
        ),
        model_width,
    )
    qkv_back, out_back, up_back, down_back, bias_back, norm_vec = back
    gain_one_b = norm_vec[:model_width]
    shift_one_b = norm_vec[model_width : 2 * model_width]
    gain_two_b = norm_vec[2 * model_width : 3 * model_width]
    shift_two_b = norm_vec[3 * model_width :]
    upstream = cotangent[0].astype(jnp.float32)
    grad_mlp = upstream.astype(jnp.bfloat16)
    grad_down_loc = jnp.einsum("ta,tb->ab", activated, grad_mlp, preferred_element_type=jnp.float32)
    grad_act = jnp.einsum("tb,ab->ta", grad_mlp, down_back, preferred_element_type=jnp.float32)
    _, gelu_pull = jax.vjp(gelu_exact, pre_act)
    grad_pre = gelu_pull(grad_act)[0].astype(jnp.bfloat16)
    grad_up_loc = jnp.einsum("ta,tb->ab", second_in, grad_pre, preferred_element_type=jnp.float32)
    grad_second = jnp.einsum("tb,ab->ta", grad_pre, up_back, preferred_element_type=jnp.float32)
    grad_after_part, grad_gain_two, grad_shift_two = norm_back(
        after_attn, gain_two_b, shift_two_b, grad_second
    )
    grad_after = upstream + grad_after_part
    grad_attn = grad_after.astype(jnp.bfloat16)
    grad_out_loc = jnp.einsum("ta,tb->ab", mixed_b, grad_attn, preferred_element_type=jnp.float32)
    grad_mixed = jnp.einsum(
        "tb,ab->ta", grad_attn, out_back, preferred_element_type=jnp.float32
    ).astype(jnp.bfloat16)
    grad_heads = grad_mixed.reshape(seq_rows, HEADS, head_dim)
    delta_rows = jnp.sum(
        grad_heads.astype(jnp.float32) * mixed_f.reshape(seq_rows, HEADS, head_dim), axis=-1
    )
    delta_heads = delta_rows.T
    stats = jnp.concatenate([log_sum.T, delta_rows], axis=1)
    all_stats = lax.all_gather(stats, "ctx", axis=0, tiled=True)
    zero_heads = jnp.zeros((HEADS, seq_rows, head_dim), jnp.float32)
    shard = (
        lax.all_gather(key_rows, "ctx", axis=0, tiled=True),
        lax.all_gather(value_rows, "ctx", axis=0, tiled=True),
    )
    shard_rows = shard[0].shape[0]
    query_block_len, query_block_count, (query_key_blocks, query_value_blocks) = to_blocks(
        shard, shard_rows
    )

    def query_one_block(total, block_in):
        key_block, value_block, position = block_in
        key_pos = position * query_block_len + jnp.arange(query_block_len, dtype=jnp.int32)
        term = query_terms(
            query_heads,
            grad_heads,
            log_sum,
            delta_heads,
            query_pos,
            query_flag,
            key_block,
            value_block,
            key_pos,
            factor,
        )
        return (total + term, None)

    def query_compute(total):
        return lax.scan(
            query_one_block,
            total,
            (query_key_blocks, query_value_blocks, jnp.arange(query_block_count, dtype=jnp.int32)),
        )[0]

    grad_q = lax.cond(jnp.int32(0) <= last_row, query_compute, keep_state, zero_heads)
    shard = (
        lax.all_gather(queries, "ctx", axis=0, tiled=True),
        lax.all_gather(grad_mixed, "ctx", axis=0, tiled=True),
    )
    shard_rows = shard[0].shape[0]
    key_block_len, key_block_count, (query_blocks, grad_blocks) = to_blocks(shard, shard_rows)

    def key_one_block(totals, block_in):
        query_block, grad_block, position = block_in
        begin = position * key_block_len
        remote_pos = begin + jnp.arange(key_block_len, dtype=jnp.int32)
        remote_flag = piece_flags(remote_pos, starts_row)
        stats_block = lax.dynamic_slice_in_dim(all_stats, begin, key_block_len, 0)
        lse_block = stats_block[:, :HEADS].T
        delta_block = stats_block[:, HEADS:].T
        grad_keys, grad_values = key_terms(
            query_block,
            grad_block,
            lse_block,
            delta_block,
            remote_pos,
            remote_flag,
            key_heads,
            value_heads,
            query_pos,
            factor,
        )
        return ((totals[0] + grad_keys, totals[1] + grad_values), None)

    def key_compute(totals):
        return lax.scan(
            key_one_block,
            totals,
            (query_blocks, grad_blocks, jnp.arange(key_block_count, dtype=jnp.int32)),
        )[0]

    grad_k, grad_v = lax.cond(
        jnp.int32(0) + shard_rows - 1 >= first_row,
        key_compute,
        keep_state,
        (zero_heads, zero_heads),
    )

    def merge_heads(grad_part):
        return (
            jnp.transpose(grad_part, (1, 0, 2)).reshape(seq_rows, model_width).astype(jnp.bfloat16)
        )

    grad_qkv_rows = jnp.concatenate(
        [merge_heads(grad_q), merge_heads(grad_k), merge_heads(grad_v)], axis=1
    )
    grad_qkv_loc = jnp.einsum(
        "ta,tb->ab", first_in, grad_qkv_rows, preferred_element_type=jnp.float32
    )
    grad_first = jnp.einsum(
        "tb,ab->ta", grad_qkv_rows, qkv_back, preferred_element_type=jnp.float32
    )
    grad_in_part, grad_gain_one, grad_shift_one = norm_back(
        inputs, gain_one_b, shift_one_b, grad_first
    )
    grad_tokens = (grad_after + grad_in_part)[None]
    grad_bias_loc = jnp.concatenate(
        [
            column_sum(grad_qkv_rows[:, :model_width]),
            column_sum(grad_qkv_rows[:, 2 * model_width :]),
            column_sum(grad_attn),
            column_sum(grad_pre),
            column_sum(grad_mlp),
        ]
    )
    grad_norm_loc = jnp.concatenate([grad_gain_one, grad_shift_one, grad_gain_two, grad_shift_two])
    summed = (
        lax.psum_scatter(grad_qkv_loc.reshape(-1), ("dp", "ctx"), scatter_dimension=0, tiled=True),
        lax.psum_scatter(grad_out_loc.reshape(-1), ("dp", "ctx"), scatter_dimension=0, tiled=True),
        lax.psum_scatter(grad_up_loc.reshape(-1), ("dp", "ctx"), scatter_dimension=0, tiled=True),
        lax.psum_scatter(grad_down_loc.reshape(-1), ("dp", "ctx"), scatter_dimension=0, tiled=True),
        lax.psum_scatter(grad_bias_loc, ("dp", "ctx"), scatter_dimension=0, tiled=True),
        lax.psum_scatter(grad_norm_loc, ("dp", "ctx"), scatter_dimension=0, tiled=True),
    )
    return (output, grad_tokens, summed[0], summed[1], summed[2], summed[3], summed[4], summed[5])


def solution(mesh):
    in_specs = (
        P("dp", "ctx", None),
        P("dp", None),
        P(("dp", "ctx")),
        P(("dp", "ctx")),
        P(("dp", "ctx")),
        P(("dp", "ctx")),
        P(("dp", "ctx")),
        P(("dp", "ctx")),
        P("dp", "ctx", None),
    )
    out_specs = (
        P("dp", "ctx", None),
        P("dp", "ctx", None),
        P(("dp", "ctx")),
        P(("dp", "ctx")),
        P(("dp", "ctx")),
        P(("dp", "ctx")),
        P(("dp", "ctx")),
        P(("dp", "ctx")),
    )
    return jax.shard_map(
        per_device, mesh=mesh, in_specs=in_specs, out_specs=out_specs, check_vma=False
    )
```

profile of v0, /device:TPU:0, one launch (start us, length us, event | category | flops | bytes accessed | tf_op | source)
XLA Modules:
  0.0 1414.9 jit_solution(3792771017945107225)
XLA Ops:
  11.6 42.1 %all-reduce = bf16[2048]{0:T(1024)(128)(2,1)S(1)} all-reduce(bf16[2048]{0:T(1024)(128)(2,1)S(1)} %dynamic-update-slice), channel_id=1, replica_groups=mesh['dp'=4,'ctx'=8] {'dp','ctx'}, use_global_device_ids=true, to_apply=%add | all-reduce | flops 2048 | bytes 8192
  53.7 65.8 %all-gather = bf16[32,1,128]{2,1,0:T(2,128)(2,1)S(1)} all-gather(bf16[1,1,128]{2,1,0:T(2,128)(2,1)} %bitcast.300), channel_id=1, replica_groups=mesh['dp'=4,'ctx'=8] {'dp','ctx'}, dimensions={0}, use_global_device_ids=true | all-gather | bytes 8448 | tf_op jit(solution)/shard_map/all_gather | solution.py:138
  131.3 68.2 %all_gather.45 = bf16[262144]{0:T(1024)(128)(2,1)S(1)} all-gather(bf16[8192]{0:T(1024)(128)(2,1)S(1)} %copy-done.33), channel_id=1, replica_groups=mesh['dp'=4,'ctx'=8] {'dp','ctx'}, dimensions={0}, use_global_device_ids=true | all-gather | bytes 540672 | tf_op jit(solution)/shard_map/all_gather | solution.py:135
  210.4 50.4 %all-gather.13.cloned.1.call-done = bf16[4096,512]{1,0:T(8,128)(2,1)} async-done(((bf16[512,512]{1,0:T(8,128)(2,1)}), bf16[4096,512]{1,0:T(8,128)(2,1)}) %all-gather.13.cloned.1.call-update) | async-done | bytes 4194320 | tf_op jit(solution)/shard_map/all_gather | solution.py:177
  260.8 6.4 copy.89
  267.2 5.8 copy.112
  273.0 62.1 %all-gather.11.cloned.1.call-done = bf16[4096,512]{1,0:T(8,128)(2,1)} async-done(((bf16[512,512]{1,0:T(8,128)(2,1)}), bf16[4096,512]{1,0:T(8,128)(2,1)}) %all-gather.11.cloned.1.call-update) | async-done | bytes 4194320 | tf_op jit(solution)/shard_map/all_gather | solution.py:176
  335.0 6.4 copy.87
  347.5 248.7 %conditional.3 = (f32[8,512]{1,0:T(8,128)}, f32[8,512]{1,0:T(8,128)}, f32[8,512,64]{1,2,0:T(8,128)}, f32[8,512]{1,0:T(8,128)S(1)}) conditional(s32[]{:T(128)} %convert_element_type.146, () %tuple.77, (s32[512]{0:T(512)S(1)}, pred[512]{0:T(512)(128)(4,1)S(1)}, bf16[16,256,8,64]{1,0,3,2:T(8,128)(2,1)S(1)}, bf16[512,8,64]{0,2,1:T(8,128)(2,1)S(1)}, ...), branch_computations={%region_3.4_spmd, %region_4.9_spmd} | conditional | flops 283409920 | bytes 50127792 | solution.py:211
  354.4 241.1 %while.45 = (s32[]{:T(128)}, f32[8,512]{1,0:T(8,128)}, f32[8,512]{1,0:T(8,128)}, f32[8,512,64]{1,2,0:T(8,128)}, s32[16]{0:T(128)S(1)}, /*index=5*/s32[512]{0:T(5...) while((s32[]{:T(128)}, f32[8,512]{1,0:T(8,128)}, ...), condition=%wide.region_8.8_spmd.clone, body=%wide.region_5.7_spmd.clone.sunk | while | flops 283408896 | bytes 33311440 | solution.py:205
  599.5 11.5 multiply_convert_fusion.1
  641.4 182.2 %conditional.4 = (f32[8,512,64]{1,2,0:T(8,128)}) conditional(s32[]{:T(128)} %convert_element_type.146, () %tuple.79, (s32[512]{0:T(512)S(1)}, pred[512]{0:T(512)(128)(4,1)S(1)}, bf16[16,256,8,64]{1,0,3,2:T(8,128)(2,1)}, bf16[512,8,64]{0,2,1:T(8,128)(2,1)S(1)}, f32[8,512]{1,0:T(8,128)S(1)}, /*index=5*/bf16[16,256,8,64]{1,0,3,2:T(8,128)(2,1)}, ...), branch_computations={%region_14.15_spmd, %region_15.18_spmd} | conditional | flops 410267136 | bytes 46196136 | solution.py:300
  641.4 5.8 copy.95
  650.6 172.9 %while.46 = (s32[]{:T(128)}, f32[8,512,64]{1,2,0:T(8,128)}, s32[16]{0:T(128)S(1)}, s32[512]{0:T(512)S(1)}, s32[512,1]{0,1:T(1,128)S(1)}, /*index=5*/s32[512,1]{0...) while((s32[]{:T(128)}, f32[8,512,64]{1,2,0:T(8,128)}, ...), condition=%wide.region_17.17_spmd.clone, body=%wide.region_16.16_spmd.clone.sunk | while | flops 410266112 | bytes 12635323 | solution.py:294
  666.8 5.5 fusion.204
  677.6 5.6 fusion.204
  688.5 5.6 fusion.204
  699.3 5.5 fusion.204
  710.1 5.5 fusion.204
  720.9 5.5 fusion.204
  731.7 5.5 fusion.204
  742.5 5.5 fusion.204
  753.3 5.5 fusion.204
  764.1 5.5 fusion.204
  785.7 5.5 fusion.204
  807.2 5.5 fusion.204
  823.6 30.9 %all_gather.50 = f32[4096,16]{0,1:T(8,128)S(1)} all-gather(f32[512,16]{0,1:T(8,128)S(1)} %pad_maximum_fusion.3), channel_id=1, replica_groups=mesh['dp'=4,'ctx'=8] {'ctx'}, dimensions={0}, use_global_device_ids=true | all-gather | bytes 294912 | tf_op jit(solution)/shard_map/all_gather | solution.py:265
  857.2 304.2 %conditional.5 = (f32[8,512,64]{1,2,0:T(8,128)}, bf16[8,512,64]{1,2,0:T(8,128)(2,1)}, f32[512]{0:T(512)S(1)}) conditional(s32[]{:T(128)} %convert_element_type.166, () %tuple.81, (bf16[4096,512]{1,0:T(8,128)(2,1)}, bf16[4096,512]{0,1:T(8,128)(2,1)}, bf16[512,512]{1,0:T(8,128)(2,1)}, bf16[512,512]{1,0:T(8,128)(2,1)}, s32[512]{0:T(512)S(1)}, ...), branch_computations={%region_18.19_spmd, %region_19.23_spmd} | conditional | flops 549995520 | bytes 56584196 | solution.py:337
  857.8 11.2 reshape.730
  869.0 9.1 copy.84
  889.0 271.4 %while.47 = (s32[]{:T(128)}, f32[8,512,64]{1,2,0:T(8,128)}, f32[8,512,64]{1,2,0:T(8,128)S(1)}, s32[512]{0:T(512)S(1)}, s32[16]{0:T(128)}, /*index=5*/s32[1,512]{...) while((s32[]{:T(128)}, f32[8,512,64]{1,2,0:T(8,128)}, ...), condition=%wide.region_22.22_spmd.clone, body=%wide.region_20.21_spmd.clone.sunk | while | flops 549208576 | bytes 19347220 | solution.py:331
  916.9 5.7 fusion.196
  933.9 5.7 fusion.196
  950.9 5.7 fusion.196
  967.9 5.7 fusion.196
  984.9 5.7 fusion.196
  1001.8 5.7 fusion.196
  1018.8 5.7 fusion.196
  1035.8 5.7 fusion.196
  1052.8 5.7 fusion.196
  1069.8 5.7 fusion.196
  1086.8 5.7 fusion.196
  1103.7 5.7 fusion.196
  1120.7 5.7 fusion.196
  1137.7 5.7 fusion.196
  1154.7 5.7 fusion.196
  1186.8 38.5 %all-reduce.7 = (f32[4096]{0:T(1024)S(1)}, f32[2048]{0:T(1024)S(1)}) all-reduce(f32[4096]{0:T(1024)S(1)} %constant_dynamic-update-slice_fusion, f32[2048]{0:T(1024)S(1)} %pad_maximum_fusion.4), channel_id=6, replica_groups=mesh['dp'=4,'ctx'=8] {'dp','ctx'}, use_global_device_ids=true, to_apply=%region_34.35.clone | all-reduce | flops 6144 | bytes 49152
  1226.5 175.3 %all-reduce.11.cloned.1.call-done = (f32[786432]{0:T(1024)}, f32[262144]{0:T(1024)}, f32[1048576]{0:T(1024)}, f32[1048576]{0:T(1024)}) async-done(((f32[786432]{0:T(1024)}, f32[262144]{0:T(1024)}, f32[1048576]{0:T(1024)}, f32[1048576]{0:T(1024)}), (f32[786432]{0:T(1024)}, f32[262144]{0:T(1024)}, f32[1048576]{0:T(1024)}, f32[1048576]{0:T(1024)})) %all-reduce.11.cloned.1.call-update) | async-done | bytes 12582928
  (669 shorter events, 625.3 us)
Async XLA Ops:
  7.2 113.8 %all-gather.9.cloned.1.call-start = ((), (), s32[]{:S(2)}) async-start(), calls=%async_computation | async-start | bytes 1622016 | tf_op jit(solution)/shard_map/all_gather | solution.py:134
  7.9 193.9 %all-gather.15.cloned.1.call-start = ((), (), s32[]{:S(2)}) async-start(), calls=%async_computation.3 | async-start | bytes 2162688 | tf_op jit(solution)/shard_map/all_gather | solution.py:136
  8.7 197.4 %all-gather.17.cloned.1.call-start = ((), (), s32[]{:S(2)}) async-start(), calls=%async_computation.4 | async-start | bytes 2162688 | tf_op jit(solution)/shard_map/all_gather | solution.py:137
  9.4 251.4 %all-gather.13.cloned.1.call-start = ((), (), s32[]{:S(2)}) async-start(), calls=%async_computation.2 | async-start | bytes 4718592 | tf_op jit(solution)/shard_map/all_gather | solution.py:177
  119.5 4.7 copy-start.22
  120.3 5.1 copy-start.26
  120.3 5.1 copy-start.24
  120.3 5.1 copy-start.40
  125.4 5.9 copy-start.33
  125.4 75.1 %copy-start.19 = (bf16[1,512,512]{2,1,0:T(8,128)(2,1)S(1)}, bf16[1,512,512]{2,1,0:T(8,128)(2,1)}, u32[]{:S(2)}) copy-start(bf16[1,512,512]{2,1,0:T(8,128)(2,1)} %param.29) | copy-start | bytes 1572868
  128.4 73.2 %copy-start.9 = (bf16[512,512]{1,0:T(8,128)(2,1)S(1)}, bf16[512,512]{1,0:T(8,128)(2,1)}, u32[]{:S(2)}) copy-start(bf16[512,512]{1,0:T(8,128)(2,1)} %get-tuple-element.1027) | copy-start | bytes 1572868
  128.4 206.6 %all-gather.11.cloned.1.call-start = ((), (), s32[]{:S(2)}) async-start(), calls=%async_computation.1 | async-start | bytes 4718592 | tf_op jit(solution)/shard_map/all_gather | solution.py:176
  130.6 726.5 %all-gather.19.cloned.1.call-start = ((), (), s32[]{:S(2)}) async-start(), calls=%async_computation.5 | async-start | bytes 4718592 | tf_op jit(solution)/shard_map/all_gather | solution.py:302
  131.2 726.0 %all-gather.21.cloned.1.call-start = ((), (), s32[]{:S(2)}) async-start(), calls=%async_computation.6 | async-start | bytes 4718592 | tf_op jit(solution)/shard_map/all_gather | solution.py:303
  200.8 423.1 %copy-start.6 = (bf16[1,512,512]{1,2,0:T(8,128)(2,1)}, bf16[1,512,512]{1,2,0:T(8,128)(2,1)S(1)}, u32[]{:S(2)}) copy-start(bf16[1,512,512]{1,2,0:T(8,128)(2,1)S(1)} %copy.93) | copy-start | bytes 1572868
  341.5 4.1 copy-start.1
  372.9 5.7 copy-start
  388.1 5.7 copy-start
  403.3 5.6 copy-start
  418.5 5.6 copy-start
  433.7 5.6 copy-start
  448.8 5.6 copy-start
  464.0 5.6 copy-start
  479.2 5.6 copy-start
  494.4 5.6 copy-start
  509.5 5.6 copy-start
  524.7 5.6 copy-start
  539.9 5.6 copy-start
  555.1 5.6 copy-start
  570.2 5.6 copy-start
  585.4 5.6 copy-start
  599.5 11.6 copy-start.13
  599.5 11.6 copy-start.20
  620.1 5.6 copy-start.8
  623.9 7.5 copy-start.30
  628.3 773.5 %all-reduce.11.cloned.1.call-start = ((), (), s32[]{:S(2)}) async-start(), calls=%async_computation.7 | async-start | bytes 25165824
  641.4 5.8 copy-start.2
  1161.4 5.2 copy-start.35
  1171.9 4.6 copy-start.18
  1176.5 5.3 copy-start.23
  1176.5 5.4 copy-start.25
  1176.5 5.6 copy-start.29
  1176.5 5.6 copy-start.27
  1182.1 4.7 copy-start.36
  1182.1 4.7 copy-start.38
  1182.1 4.7 copy-start.37
  1182.1 4.7 copy-start.34
  1182.1 4.7 copy-start.41
  (18 other events, 38.9 us)
Sparse Core Ops, SparseCore 0:
  10.9 57.8 all-gather.8
  71.7 55.3 all-gather.14
  130.2 56.2 all-gather.16
  188.4 72.3 all-gather.12
  263.3 71.6 all-gather.10
  337.0 71.6 all-gather.18
  628.5 73.0 all-gather.20
  1171.3 230.4 all-reduce.10
where the time goes:
time: 1430 us; the launch traced here: 1410 us
  matrix products  510 us (36%)
  waiting for transfers between devices  290 us (20%)
  blocking collectives  245 us (17%)
  local copies, waits for them, and re-layouts  180 us (13%)
  other arithmetic  141 us (10%)
  loops' own time  33.2 us (2%)
  between operations  14.9 us (1%)
    unnamed x9, waiting for transfers between devices  178 us
    dot_general x16, matrix products, key_terms(): jnp.einsum('hqk,qhd->hkd', dscores, query_block, preferred_element_type=j...  91 us
    dot_general x16, matrix products, query_terms(): jnp.einsum('hqk,khd->hqd', dscores, key_block, preferred_element_type=jnp...  88 us
    unnamed x2, blocking collectives  80.6 us
    all_gather x1, blocking collectives, per_device(): lax.all_gather(out_weight, ('dp', 'ctx'), axis=0, tiled=True)  68.2 us
    all_gather x1, blocking collectives, per_device(): lax.all_gather(biases, ('dp', 'ctx'), axis=0, tiled=True)  65.8 us
    all_gather x1, waiting for transfers between devices, per_device(): lax.all_gather(key_rows, 'ctx', axis=0, tiled=True)  62.1 us
    dot_general x16, matrix products, query_terms(): jnp.einsum('qhd,khd->hqk', query_heads, key_block, preferred_element_type...  60.4 us
  transfers between devices with their start and end apart: 8, of which 3 were waited for; matrix products, arithmetic and copies ran while one was open for 36% of the time, Pallas kernels for 0%

commit v1 on v0

--- a/solution.py
+++ b/solution.py
@@ -1,6 +1,11 @@
+import functools
+import math
+
 import jax
 import jax.numpy as jnp
 from jax import lax
+from jax.experimental import pallas as pl
+from jax.experimental.pallas import tpu as pltpu
 from jax.sharding import PartitionSpec as P
 
 HEADS = 8
@@ -124,7 +129,7 @@
     return (grad_keys, grad_values)
 
 
-def per_device(
+def general_device(
     tokens, piece_starts, qkv_weight, out_weight, up_weight, down_weight, biases, norms, cotangent
 ):
     model_width = tokens.shape[2]
@@ -380,28 +385,1084 @@
     return (output, grad_tokens, summed[0], summed[1], summed[2], summed[3], summed[4], summed[5])
 
 
+MESH = pl.DeviceIdType.MESH
+BF16 = jnp.bfloat16
+F32 = jnp.float32
+VMEM_SPEC = pl.BlockSpec(memory_space=pltpu.VMEM)
+SMEM_SPEC = pl.BlockSpec(memory_space=pltpu.SMEM)
+ANY_SPEC = pl.BlockSpec(memory_space=pl.ANY)
+HALF = 64
+NT = (((1,), (1,)), ((), ()))
+TN = (((0,), (0,)), ((), ()))
+VMEM_LIMIT = 60 << 20
+
+
+def params(cid=None):
+    if cid is None:
+        return pltpu.CompilerParams(vmem_limit_bytes=VMEM_LIMIT)
+    return pltpu.CompilerParams(
+        collective_id=cid, has_side_effects=True, vmem_limit_bytes=VMEM_LIMIT
+    )
+
+
+def place():
+    dp = lax.axis_index("dp")
+    ctx = lax.axis_index("ctx")
+    return dp // 2, dp % 2, ctx // 2, ctx % 2
+
+
+def device(x, core, z, y):
+    return (x * 2 + core, z * 2 + y)
+
+
+def greet(peers):
+    barrier = pltpu.get_barrier_semaphore()
+    for peer in peers:
+        pl.semaphore_signal(barrier, inc=1, device_id=peer, device_id_type=MESH)
+    pl.semaphore_wait(barrier, len(peers))
+
+
+def remote(src, dst, send, recv, peer):
+    return pltpu.make_async_remote_copy(
+        src_ref=src,
+        dst_ref=dst,
+        send_sem=send,
+        recv_sem=recv,
+        device_id=peer,
+        device_id_type=MESH,
+    )
+
+
+def mm(a, b, dims=None):
+    if dims is None:
+        return jnp.dot(a, b, preferred_element_type=F32)
+    return lax.dot_general(a, b, dims, preferred_element_type=F32)
+
+
+def swap_halves(v):
+    return jnp.concatenate([v[:, HALF:], v[:, :HALF]], axis=1)
+
+
+def left_lanes(rows):
+    return lax.broadcasted_iota(jnp.int32, (rows, 2 * HALF), 1) < HALF
+
+
+def diagonal_mask(size, flags, first, transposed):
+    row = lax.broadcasted_iota(jnp.int32, (size, size), 0)
+    col = lax.broadcasted_iota(jnp.int32, (size, size), 1)
+    key, query = (row, col) if transposed else (col, row)
+    allowed = key <= query
+    same = (key // PIECE) == (query // PIECE)
+    for t in range(size // PIECE):
+        inside = jnp.logical_and(same, (query // PIECE) == t)
+        allowed = jnp.logical_or(allowed, jnp.logical_and(inside, flags[first + t] > 0))
+    return allowed
+
+
+def xor8(a, b):
+    return (
+        (a // 4 + b // 4) % 2 * 4 + (a // 2 % 2 + b // 2 % 2) % 2 * 2 + (a % 2 + b % 2) % 2
+    )
+
+
+def unflatten(flat_ref, stage, rows, groups):
+    count = rows * groups
+    stage[pl.ds(0, count), :] = flat_ref[...].astype(F32)
+    return [stage[pl.ds(j, rows, stride=groups), :] for j in range(groups)]
+
+
+def forward_kernel(
+    flags,
+    tokens,
+    small,
+    qkv_flat,
+    out_flat,
+    up_flat,
+    down_flat,
+    a1_ref,
+    got,
+    mix,
+    o_ref,
+    lse_ref,
+    vec_ref,
+    qkv_all,
+    ou_all,
+    down_all,
+    stage,
+    qkv_own,
+    ou_own,
+    down_own,
+    norm_s,
+    packed,
+    q_s,
+    k_s,
+    v_s,
+    m_s,
+    acc_s,
+    o2_s,
+    g_own,
+    g_send,
+    g_recv,
+    x_send,
+    x_recv,
+    o_send,
+    o_recv,
+):
+    x, core, z, y = place()
+    ox, oc, oy = 1 - x, 1 - core, 1 - y
+    me = z * 2 + y
+    width = tokens.shape[1]
+    rows = tokens.shape[0]
+    half = rows // 2
+    tile = 2 * rows
+    groups = width // 128
+    scale = math.log2(math.e) * HALF**-0.5
+    left = left_lanes(rows)
+    left_half = left_lanes(half)
+    to_x = device(ox, core, z, y)
+    to_y = device(x, core, z, oy)
+    to_core = device(x, oc, z, y)
+    others = [(z + j) % 4 for j in range(1, 4)]
+
+    qkv = unflatten(qkv_flat, stage, 16, 3 * groups)
+    left16 = left_lanes(16)
+    for j in range(groups):
+        k_pair, v_pair = qkv[groups + j], qkv[2 * groups + j]
+        at = 128 * j
+        qkv_own[:, at : at + 128] = qkv[j].astype(BF16)
+        at = 128 * (groups + 2 * j)
+        qkv_own[:, at : at + 128] = jnp.where(left16, k_pair, swap_halves(v_pair)).astype(BF16)
+        at += 128
+        qkv_own[:, at : at + 128] = jnp.where(left16, swap_halves(k_pair), v_pair).astype(BF16)
+    qkv_own[:, 3 * width :] = small[...]
+    greet(
+        [device(x, core, z2, y2) for z2 in [z] + others for y2 in (y, oy)][1:] + [to_x, to_core]
+    )
+
+    arrays = ((qkv_own, qkv_all), (ou_own, ou_all), (down_own, down_all))
+
+    def moves(phase, a):
+        own, full = arrays[a]
+        if phase == 1:
+            mine = full.at[x, core, z, y]
+            return [(own, mine, device(x, core, o, y), j) for j, o in enumerate(others)]
+        if phase == 2:
+            part = full.at[x, core, :, y]
+            return [(part, part, to_x, 3), (part, part, to_y, 4), (part, part, to_core, 5)]
+        if phase == 3:
+            low = full.at[x, core, pl.ds(0, 2), oy]
+            high = full.at[ox, core, pl.ds(2, 2), y]
+            from_x = full.at[ox, core, :, y]
+            from_y = full.at[x, core, :, oy]
+            return [
+                (low, low, to_x, 6),
+                (high, high, to_y, 7),
+                (from_x, from_x, to_core, 8),
+                (from_y, from_y, to_core, 9),
+            ]
+        part = full.at[ox, core, :, oy]
+        return [(part, part, to_core, 10)]
+
+    def phase_copies(phase, a):
+        copies = [
+            remote(src, dst, g_send.at[a * 11 + n], g_recv.at[a * 11 + n], peer)
+            for src, dst, peer, n in moves(phase, a)
+        ]
+        if phase == 1:
+            own, full = arrays[a]
+            copies.append(pltpu.make_async_copy(own, full.at[x, core, z, y], g_own.at[a]))
+        return copies
+
+    def launch(phase, a):
+        for copy in phase_copies(phase, a):
+            copy.start()
+
+    def finish(phase, a):
+        for copy in phase_copies(phase, a):
+            copy.wait()
+
+    launch(1, 0)
+    out_parts = unflatten(out_flat, stage, 16, groups)
+    for j in range(groups):
+        ou_own[:, 128 * j : 128 * (j + 1)] = out_parts[j].astype(BF16)
+    up_groups = up_flat.shape[0] // 16
+    up_parts = unflatten(up_flat, stage, 16, up_groups)
+    for j in range(up_groups):
+        at = width + 128 * j
+        ou_own[:, at : at + 128] = up_parts[j].astype(BF16)
+    down_rows = down_flat.shape[0] // groups
+    down_parts = unflatten(down_flat, stage, down_rows, groups)
+    for j in range(groups):
+        down_own[:, 128 * j : 128 * (j + 1)] = down_parts[j].astype(BF16)
+    finish(1, 0)
+    launch(2, 0)
+    value = tokens[...].astype(F32)
+    center = jnp.mean(value, axis=1, keepdims=True)
+    offset = value - center
+    spread = jnp.mean(offset * offset, axis=1, keepdims=True)
+    norm_s[...] = offset * lax.rsqrt(spread + eps_norm)
+    finish(2, 0)
+    launch(3, 0)
+    finish(3, 0)
+    launch(4, 0)
+    finish(4, 0)
+
+    vec_ref[...] = jnp.zeros_like(vec_ref)
+    devices = [(a, b, c, d) for a in range(2) for b in range(2) for c in range(4) for d in range(2)]
+    norm_rows = []
+    for n, (a, b, c, d) in enumerate(devices):
+        piece = qkv_all[a, b, c, d, :, pl.ds(3 * width, 128)].astype(F32)
+        vec_ref[0:1, 128 * n : 128 * (n + 1)] = piece[0:1]
+        norm_rows.append(piece[1:2, :HALF])
+    base = 128 * len(devices)
+    for n in range(len(devices) // 2):
+        pair = jnp.concatenate([norm_rows[2 * n], norm_rows[2 * n + 1]], axis=1)
+        vec_ref[0:1, base + 128 * n : base + 128 * (n + 1)] = pair
+    gain = vec_ref[0:1, base : base + width]
+    shift = vec_ref[0:1, base + width : base + 2 * width]
+    a1_ref[...] = (norm_s[...] * gain + shift).astype(BF16)
+
+    hz = z // 2
+    order = ((1 - hz) * 2 + z % 2, (1 - hz) * 2 + 1 - z % 2, hz * 2 + 1 - z % 2, z)
+    marks = (4, 6, 2, 0)
+    left1 = left_lanes(1)
+    for tz, mark in zip(order, marks):
+        a1 = a1_ref[...]
+        at = pl.multiple_of(128 * tz, 128)
+        w_q = qkv_all[:, :, :, :, :, pl.ds(at, 128)].reshape(width, 128)
+        q = (mm(a1, w_q) + vec_ref[0:1, pl.ds(at, 128)]).astype(BF16)
+        at_kv = pl.multiple_of(width + 256 * tz, 128)
+        w_kv = qkv_all[:, :, :, :, :, pl.ds(at_kv, 256)].reshape(width, 256)
+        bias = vec_ref[0:1, pl.ds(pl.multiple_of(width + 128 * tz, 128), 128)]
+        kv = mm(a1, w_kv)
+        even = kv[:, :128] + jnp.where(left1, 0.0, swap_halves(bias))
+        odd = kv[:, 128:] + jnp.where(left1, 0.0, bias)
+        packed[2 * tz, :rows] = even.astype(BF16)
+        packed[2 * tz + 1, :rows] = odd.astype(BF16)
+        top, low = q[:half], q[half:]
+        packed[2 * tz, rows:] = jnp.where(left_half, top, swap_halves(low))
+        packed[2 * tz + 1, rows:] = jnp.where(left_half, swap_halves(top), low)
+        for step in range(2):
+            ty = (y + step) % 2
+            index = mark + step
+            src = packed.at[2 * tz + ty]
+            if index == 0:
+                pltpu.make_async_copy(src, got.at[me], x_recv.at[0]).start()
+            else:
+                remote(
+                    src, got.at[me], x_send.at[index], x_recv.at[index], device(x, core, tz, ty)
+                ).start()
+    launch(1, 1)
+    launch(1, 2)
+
+    def block_wait(sems, index, view):
+        pltpu.make_async_copy(view, view, sems.at[index]).wait()
+
+    @pl.loop(0, 4)
+    def _(i):
+        for t in range(2):
+            b = 2 * i + t
+            block_wait(x_recv, xor8(b, me), got.at[b])
+            at = pl.multiple_of(b * rows, rows)
+            pair = got[b, :rows]
+            k_s[pl.ds(at, rows), :] = jnp.where(left, pair, 0).astype(BF16)
+            v_s[pl.ds(at, rows), :] = jnp.where(left, 1, pair).astype(BF16)
+            both = got[b, rows:]
+            q_s[pl.ds(at, half), :] = jnp.where(left_half, both, 0).astype(BF16)
+            q_s[pl.ds(at + half, half), :] = jnp.where(left_half, swap_halves(both), 0).astype(
+                BF16
+            )
+
+        @pl.when(i == 1)
+        def _():
+            for a in (1, 2):
+                finish(1, a)
+                launch(2, a)
+
+        @pl.when(i == 2)
+        def _():
+            for a in (1, 2):
+                finish(2, a)
+                launch(3, a)
+
+        @pl.when(i == 3)
+        def _():
+            for a in (1, 2):
+                finish(3, a)
+                launch(4, a)
+
+        at = pl.multiple_of(i * tile, tile)
+        q = q_s[pl.ds(at, tile), :]
+        s = mm(q, k_s[pl.ds(at, tile), :], NT)
+        allowed = diagonal_mask(tile, flags, i * (tile // PIECE), False)
+        s = jnp.where(allowed, s, masked_score)
+        m = jnp.max(s, axis=1, keepdims=True) * scale
+        p = jnp.exp2(s * scale - m)
+        m_s[...] = jnp.broadcast_to(m, m_s.shape)
+        acc_s[...] = mm(p.astype(BF16), v_s[pl.ds(at, tile), :])
+
+        @pl.loop(0, i)
+        def _(j):
+            begin = pl.multiple_of(j * tile, tile)
+            s = mm(q_s[pl.ds(at, tile), :], k_s[pl.ds(begin, tile), :], NT)
+            old = m_s[...]
+            new = jnp.maximum(old, jnp.max(s, axis=1, keepdims=True) * scale)
+            p = jnp.exp2(s * scale - new[:, :1])
+            m_s[...] = new
+            acc_s[...] = acc_s[...] * jnp.exp2(old - new) + mm(
+                p.astype(BF16), v_s[pl.ds(begin, tile), :]
+            )
+
+        acc = acc_s[...]
+        total = jnp.broadcast_to(acc[:, :1], acc.shape)
+        o = acc / total
+        o_ref[pl.ds(at, tile), :] = o
+        lse = m_s[...] + jnp.log2(total)
+        lse_ref[:, pl.ds(at, tile)] = jnp.transpose(lse)[:8]
+        for t in range(2):
+            b = 2 * i + t
+            top = o[t * rows : t * rows + half]
+            low = o[t * rows + half : (t + 1) * rows]
+            o2_s[b] = jnp.where(left_half, swap_halves(top), low).astype(BF16)
+            index = xor8(b, me)
+
+            @pl.when(b == me)
+            def _():
+                pltpu.make_async_copy(o2_s.at[b], mix.at[me], o_recv.at[0]).start()
+
+            @pl.when(b != me)
+            def _():
+                remote(
+                    o2_s.at[b],
+                    mix.at[me],
+                    o_send.at[index],
+                    o_recv.at[index],
+                    device(x, core, i, t),
+                ).start()
+
+    for a in (1, 2):
+        finish(4, a)
+    for index in range(8):
+        block_wait(o_recv, index, mix.at[0])
+        if index:
+            block_wait(x_send, index, packed.at[0])
+            block_wait(o_send, index, o2_s.at[0])
+
+
+def forward(flags, tokens, small, qkv_flat, out_flat, up_flat, down_flat, cid):
+    rows, width = tokens.shape
+    length = rows * HEADS
+    hidden = up_flat.shape[0] * 128 // 16
+    down_rows = down_flat.shape[0] * 128 // width
+    lanes = 2 * HALF
+    every = (2, 2, 4, 2)
+    vmem = pltpu.VMEM
+    dma = pltpu.SemaphoreType.DMA
+    return pl.pallas_call(
+        forward_kernel,
+        out_shape=[
+            jax.ShapeDtypeStruct((rows, width), BF16),
+            jax.ShapeDtypeStruct((HEADS, rows + rows // 2, lanes), BF16),
+            jax.ShapeDtypeStruct((HEADS, rows // 2, lanes), BF16),
+            jax.ShapeDtypeStruct((length, lanes), F32),
+            jax.ShapeDtypeStruct((8, length), F32),
+            jax.ShapeDtypeStruct((8, 4096 + 4 * width), F32),
+            jax.ShapeDtypeStruct(every + (16, 3 * width + 128), BF16),
+            jax.ShapeDtypeStruct(every + (16, width + hidden), BF16),
+            jax.ShapeDtypeStruct(every + (down_rows, width), BF16),
+        ],
+        in_specs=[SMEM_SPEC] + [VMEM_SPEC] * 6,
+        out_specs=[VMEM_SPEC] * 7 + [ANY_SPEC] * 2,
+        scratch_shapes=[
+            vmem((256, 128), F32),
+            vmem((16, 3 * width + 128), BF16),
+            vmem((16, width + hidden), BF16),
+            vmem((down_rows, width), BF16),
+            vmem((rows, width), F32),
+            vmem((HEADS, rows + rows // 2, lanes), BF16),
+            vmem((length, lanes), BF16),
+            vmem((length, lanes), BF16),
+            vmem((length, lanes), BF16),
+            vmem((2 * rows, lanes), F32),
+            vmem((2 * rows, lanes), F32),
+            vmem((HEADS, rows // 2, lanes), BF16),
+            dma((3,)),
+            dma((33,)),
+            dma((33,)),
+            dma((8,)),
+            dma((8,)),
+            dma((8,)),
+            dma((8,)),
+        ],
+        compiler_params=params(cid),
+    )(flags, tokens, small, qkv_flat, out_flat, up_flat, down_flat)
+
+
+def middle_kernel(
+    tokens,
+    cot,
+    mix,
+    vec,
+    ou_all,
+    down_all,
+    out_ref,
+    dx_ref,
+    do2_ref,
+    acc_ou,
+    acc_down,
+    sums_ref,
+    o_s,
+    x1_s,
+    n2_s,
+    a2_s,
+    gl_s,
+    du_s,
+    dh_s,
+    da_s,
+    r_s,
+    send2,
+    core_ou,
+    core_down,
+    got_ou,
+    got_down,
+    x_send,
+    x_recv,
+    c_send,
+    c_recv,
+):
+    x, core, z, y = place()
+    oc, oy = 1 - core, 1 - y
+    me = z * 2 + y
+    rows, width = tokens.shape
+    half = rows // 2
+    hidden = ou_all.shape[-1] - width
+    left_half = left_lanes(half)
+    to_core = device(x, oc, z, y)
+    every = (2, 2, 4, 2)
+    greet(
+        [device(x, core, (z + a) % 4, (y + b) % 2) for a in range(4) for b in range(2)][1:]
+        + [to_core]
+    )
+    bias_o = vec[0:1, 2 * width : 3 * width]
+    bias_down = vec[0:1, 3 * width + hidden : 4 * width + hidden]
+    base = 4 * width + hidden
+    gain = vec[0:1, base + 2 * width : base + 3 * width]
+    shift = vec[0:1, base + 3 * width : base + 4 * width]
+
+    for j in range(HEADS // 2):
+        even, odd = mix[2 * j], mix[2 * j + 1]
+        at = 128 * j
+        o_s[:half, at : at + 128] = jnp.where(left_half, even, swap_halves(odd))
+        o_s[half:, at : at + 128] = jnp.where(left_half, swap_halves(even), odd)
+    w_out = ou_all[:, :, :, :, :, :width].reshape(width, width)
+    x1 = tokens[...].astype(F32) + mm(o_s[...], w_out) + bias_o
+    x1_s[...] = x1
+    center = jnp.mean(x1, axis=1, keepdims=True)
+    offset = x1 - center
+    spread = jnp.mean(offset * offset, axis=1, keepdims=True)
+    inverse = lax.rsqrt(spread + eps_norm)
+    r_s[...] = jnp.broadcast_to(inverse, r_s.shape)
+    n2 = offset * inverse
+    n2_s[...] = n2
+    a2_s[...] = (n2 * gain + shift).astype(BF16)
+    sums_ref[...] = jnp.zeros_like(sums_ref)
+
+    @pl.loop(0, hidden // width)
+    def _(j):
+        at = pl.multiple_of(j * width, width)
+        w_up = ou_all[:, :, :, :, :, pl.ds(pl.multiple_of(width + at, width), width)].reshape(
+            width, width
+        )
+        b_up = vec[0:1, pl.ds(pl.multiple_of(3 * width + at, width), width)]
+        w_down = down_all[j // 2, j % 2].reshape(width, width)
+        u = mm(a2_s[...], w_up) + b_up
+        phi = 0.5 * (1.0 + lax.erf(u * (0.5**0.5)))
+        slope = phi + u * jnp.exp(-0.5 * u * u) * (1.0 / math.sqrt(2.0 * math.pi))
+        gl_s[:, pl.ds(at, width)] = (u * phi).astype(BF16)
+        grad = mm(cot[...], w_down, NT)
+        du = (grad * slope).astype(BF16)
+        du_s[:, pl.ds(at, width)] = du
+        sums_ref[0:1, pl.ds(pl.multiple_of(3 * width + at, width), width)] = jnp.sum(
+            du.astype(F32), axis=0, keepdims=True
+        )
+        part = mm(du, w_up, NT)
+
+        @pl.when(j == 0)
+        def _():
+            dh_s[...] = part
+
+        @pl.when(j > 0)
+        def _():
+            dh_s[...] += part
+
+    dh2 = dh_s[...]
+    n2 = n2_s[...]
+    sums_ref[0:1, base + 2 * width : base + 3 * width] = jnp.sum(dh2 * n2, axis=0, keepdims=True)
+    sums_ref[0:1, base + 3 * width : base + 4 * width] = jnp.sum(dh2, axis=0, keepdims=True)
+    e = dh2 * gain
+    mean_e = jnp.mean(e, axis=1, keepdims=True)
+    mean_en = jnp.mean(e * n2, axis=1, keepdims=True)
+    dx = cot[...].astype(F32) + r_s[:, :1] * (e - mean_e - n2 * mean_en)
+    dx_ref[...] = dx
+    da = dx.astype(BF16)
+    da_s[...] = da
+    w_out = ou_all[:, :, :, :, :, :width].reshape(width, width)
+    grad_o = mm(da, w_out, NT).astype(BF16)
+    for j in range(HEADS // 2):
+        group = grad_o[:, 128 * j : 128 * (j + 1)]
+        top, low = group[:half], group[half:]
+        send2[2 * j] = jnp.where(left_half, top, swap_halves(low))
+        send2[2 * j + 1] = jnp.where(left_half, swap_halves(top), low)
+    hz = z // 2
+    order = ((1 - hz) * 2 + z % 2, (1 - hz) * 2 + 1 - z % 2, hz * 2 + 1 - z % 2, z)
+    for tz, mark in zip(order, (4, 6, 2, 0)):
+        for step in range(2):
+            ty = (y + step) % 2
+            index = mark + step
+            src = send2.at[2 * tz + ty]
+            if index == 0:
+                pltpu.make_async_copy(src, do2_ref.at[me], x_recv.at[0]).start()
+            else:
+                remote(
+                    src,
+                    do2_ref.at[me],
+                    x_send.at[index],
+                    x_recv.at[index],
+                    device(x, core, tz, ty),
+                ).start()
+
+    def grads(c, n):
+        dp = 2 * n + c
+        at = pl.multiple_of(dp * 128, 128)
+        down_at = pl.multiple_of(dp * width, width)
+        d_down = mm(gl_s[:, pl.ds(down_at, width)], cot[...], TN)
+        d_up = mm(a2_s[:, pl.ds(at, 128)], du_s[...], TN)
+        d_out = mm(o_s[:, pl.ds(at, 128)], da_s[...], TN)
+        return (
+            d_down.reshape(4, 2, width // 8, width),
+            d_up.reshape(4, 2, 16, hidden),
+            d_out.reshape(4, 2, 16, width),
+        )
+
+    for n in range(2):
+        d_down, d_up, d_out = grads(oc, n)
+        core_down[n] = d_down.astype(BF16)
+        core_ou[n, :, :, :, width:] = d_up.astype(BF16)
+        core_ou[n, :, :, :, :width] = d_out.astype(BF16)
+    to_ou = remote(core_ou, got_ou, c_send.at[0], c_recv.at[0], to_core)
+    to_down = remote(core_down, got_down, c_send.at[1], c_recv.at[1], to_core)
+    to_ou.start()
+    to_down.start()
+    sums_ref[0:1, 2 * width : 3 * width] = jnp.sum(da_s[...].astype(F32), axis=0, keepdims=True)
+    sums_ref[0:1, 3 * width + hidden : 4 * width + hidden] = jnp.sum(
+        cot[...].astype(F32), axis=0, keepdims=True
+    )
+    result = x1_s[...] + mm(gl_s[...], down_all[...].reshape(hidden, width)) + bias_down
+    out_ref[...] = result.astype(BF16)
+    for n in range(2):
+        d_down, d_up, d_out = grads(core, n)
+        acc_down[n] = d_down
+        acc_ou[n, :, :, :, width:] = d_up
+        acc_ou[n, :, :, :, :width] = d_out
+    to_ou.wait()
+    to_down.wait()
+    acc_ou[...] += got_ou[...].astype(F32)
+    acc_down[...] += got_down[...].astype(F32)
+    for index in range(8):
+        pltpu.make_async_copy(do2_ref.at[0], do2_ref.at[0], x_recv.at[index]).wait()
+        if index:
+            pltpu.make_async_copy(send2.at[0], send2.at[0], x_send.at[index]).wait()
+
+
+def middle(tokens, cot, mix, vec, ou_all, down_all, cid):
+    rows, width = tokens.shape
+    hidden = ou_all.shape[-1] - width
+    lanes = 2 * HALF
+    vmem = pltpu.VMEM
+    dma = pltpu.SemaphoreType.DMA
+    ou = (2, 4, 2, 16, width + hidden)
+    down = (2, 4, 2, hidden // 32, width)
+    return pl.pallas_call(
+        middle_kernel,
+        out_shape=[
+            jax.ShapeDtypeStruct((rows, width), BF16),
+            jax.ShapeDtypeStruct((rows, width), F32),
+            jax.ShapeDtypeStruct((HEADS, rows // 2, lanes), BF16),
+            jax.ShapeDtypeStruct(ou, F32),
+            jax.ShapeDtypeStruct(down, F32),
+            jax.ShapeDtypeStruct(vec.shape, F32),
+        ],
+        in_specs=[VMEM_SPEC] * 6,
+        out_specs=[VMEM_SPEC] * 6,
+        scratch_shapes=[
+            vmem((rows, width), BF16),
+            vmem((rows, width), F32),
+            vmem((rows, width), F32),
+            vmem((rows, width), BF16),
+            vmem((rows, hidden), BF16),
+            vmem((rows, hidden), BF16),
+            vmem((rows, width), F32),
+            vmem((rows, width), BF16),
+            vmem((rows, lanes), F32),
+            vmem((HEADS, rows // 2, lanes), BF16),
+            vmem(ou, BF16),
+            vmem(down, BF16),
+            vmem(ou, BF16),
+            vmem(down, BF16),
+            dma((8,)),
+            dma((8,)),
+            dma((2,)),
+            dma((2,)),
+        ],
+        compiler_params=params(cid),
+    )(tokens, cot, mix, vec, ou_all, down_all)
+
+
+def reduce_buffers(rows, width, wire):
+    vmem = pltpu.VMEM
+    return [
+        vmem((2, 2, rows, width), wire),
+        vmem((2, 2, rows, width), wire),
+        vmem((2, 2, rows, width), wire),
+        vmem((2, 2, rows, width), wire),
+        vmem((2, 2, rows, width), wire),
+        vmem((2, 2, rows, width), wire),
+        vmem((4, rows, width), wire),
+        vmem((3, rows, width), wire),
+        vmem((4, rows, width), F32),
+    ]
+
+
+REDUCE_BUFFERS = 9
+REDUCE_COPIES = 7
+
+
+def reducer(acc, bufs, send, recv, first):
+    to_wire_x, from_x, to_wire_y, from_y, to_two, from_two, to_three, from_three, total = bufs
+    wire = to_wire_x.dtype
+    x, core, z, y = place()
+    ox, oy = 1 - x, 1 - y
+    to_x = device(ox, core, z, y)
+    to_y = device(x, core, z, oy)
+    others = [(z + j) % 4 for j in range(1, 4)]
+
+    def copies(stage):
+        def make(n, src, dst, peer):
+            return remote(src, dst, send.at[first + n], recv.at[first + n], peer)
+
+        if stage == 1:
+            return [make(0, to_wire_x, from_x, to_x), make(1, to_wire_y, from_y, to_y)]
+        if stage == 2:
+            return [
+                make(2, to_two.at[0], from_two.at[0], to_y),
+                make(3, to_two.at[1], from_two.at[1], to_x),
+            ]
+        return [
+            make(4 + j, to_three.at[other], from_three.at[j], device(x, core, other, y))
+            for j, other in enumerate(others)
+        ]
+
+    def launch(stage):
+        if stage == 1:
+            to_wire_x[...] = acc[ox, pl.ds(0, 2)].astype(wire)
+            for n in range(2):
+                to_wire_y[n] = acc[n, pl.ds(2, 2), oy].astype(wire)
+        elif stage == 2:
+            to_two[0] = (acc[x, pl.ds(0, 2), oy] + from_x[:, oy].astype(F32)).astype(wire)
+            to_two[1] = (acc[ox, pl.ds(2, 2), y] + from_y[ox].astype(F32)).astype(wire)
+        else:
+            low = acc[x, pl.ds(0, 2), y] + from_x[:, y].astype(F32) + from_two[0].astype(F32)
+            high = acc[x, pl.ds(2, 2), y] + from_y[x].astype(F32) + from_two[1].astype(F32)
+            total[pl.ds(0, 2)] = low
+            total[pl.ds(2, 2)] = high
+            to_three[pl.ds(0, 2)] = low.astype(wire)
+            to_three[pl.ds(2, 2)] = high.astype(wire)
+        for copy in copies(stage):
+            copy.start()
+
+    def finish(stage):
+        for copy in copies(stage):
+            copy.wait()
+
+    def result():
+        value = total[z]
+        for j in range(3):
+            value = value + from_three[j].astype(F32)
+        return value
+
+    return launch, finish, result
+
+
+def reduce_peers():
+    x, core, z, y = place()
+    return [device(x, core, (z + j) % 4, y) for j in range(1, 4)] + [
+        device(1 - x, core, z, y),
+        device(x, core, z, 1 - y),
+    ]
+
+
+def backward_kernel(*refs):
+    flags, got, do2_ref, o_ref, lse_ref, acc_ou, acc_down = refs[:7]
+    grads, sum_ou, sum_down = refs[7:10]
+    packed, qd_s, k_s, v_s, delta_s, dq_s, dkv_s = refs[10:17]
+    bufs_ou = refs[17 : 17 + REDUCE_BUFFERS]
+    bufs_down = refs[17 + REDUCE_BUFFERS : 17 + 2 * REDUCE_BUFFERS]
+    r_send, r_recv, x_send, x_recv = refs[17 + 2 * REDUCE_BUFFERS :]
+    x, core, z, y = place()
+    me = z * 2 + y
+    blocks = got.shape[0]
+    rows = got.shape[1] // 3 * 2
+    half = rows // 2
+    scale = math.log2(math.e) * HALF**-0.5
+    left = left_lanes(rows)
+    left_half = left_lanes(half)
+    greet(
+        [device(x, core, (z + a) % 4, (y + b) % 2) for a in range(4) for b in range(2)][1:]
+        + [device(1 - x, core, z, y)]
+    )
+    sums = (
+        reducer(acc_ou, bufs_ou, r_send, r_recv, 0),
+        reducer(acc_down, bufs_down, r_send, r_recv, REDUCE_COPIES),
+    )
+    for launch, _, _ in sums:
+        launch(1)
+
+    @pl.loop(0, blocks)
+    def _(b):
+        at = pl.multiple_of(b * rows, rows)
+        pair = got[b, :rows]
+        k_s[pl.ds(at, rows), :] = jnp.where(left, pair, 0).astype(BF16)
+        v_s[pl.ds(at, rows), :] = jnp.where(left, 0, pair).astype(BF16)
+        both = got[b, rows:]
+        grad = do2_ref[b]
+        top = jnp.where(left_half, both, swap_halves(grad))
+        low = jnp.where(left_half, swap_halves(both), grad)
+        qd_s[pl.ds(at, half), :] = top
+        qd_s[pl.ds(at + half, half), :] = low
+        for part, begin in ((top, 0), (low, half)):
+            product = jnp.where(
+                left_half, 0.0, part.astype(F32) * o_ref[pl.ds(at + begin, half), :]
+            )
+            delta = jnp.sum(jnp.transpose(product), axis=0, keepdims=True)
+            delta_s[:, pl.ds(at + begin, half)] = jnp.broadcast_to(delta, (8, half))
+        dq_s[pl.ds(at, rows), :] = jnp.zeros((rows, 2 * HALF), F32)
+        dkv_s[pl.ds(at, rows), :] = jnp.zeros((rows, 2 * HALF), F32)
+
+    def tile(kj, qi, diagonal):
+        k0 = pl.multiple_of(kj * rows, rows)
+        q0 = pl.multiple_of(qi * rows, rows)
+        k = k_s[pl.ds(k0, rows), :]
+        v = v_s[pl.ds(k0, rows), :]
+        qd = qd_s[pl.ds(q0, rows), :]
+        scores = mm(k, qd, NT)
+        dprobs = mm(v, qd, NT)
+        p = jnp.exp2(scores * scale - lse_ref[:1, pl.ds(q0, rows)])
+        if diagonal:
+            allowed = diagonal_mask(rows, flags, kj * (rows // PIECE), True)
+            p = jnp.where(allowed, p, 0.0)
+        ds = (p * (dprobs - delta_s[:1, pl.ds(q0, rows)])).astype(BF16)
+        dkv_s[pl.ds(k0, rows), :] += jnp.where(left, mm(ds, qd), mm(p.astype(BF16), qd))
+        dq_s[pl.ds(q0, rows), :] += mm(ds, k, TN)
+
+    down = 1 - me // (blocks // 2)
+
+    @pl.loop(0, blocks)
+    def _(t):
+        a = down * (blocks - 1 - t) + (1 - down) * t
+        for stage, step in ((1, 2), (2, 4)):
+
+            @pl.when(t == step)
+            def _():
+                for _, finish, _ in sums:
+                    finish(stage)
+                for launch, _, _ in sums:
+                    launch(stage + 1)
+
+        tile(a, a, True)
+
+        @pl.loop(0, blocks - 1 - t)
+        def _(u):
+            b = down * u + (1 - down) * (a + 1 + u)
+            tile(down * b + (1 - down) * a, down * a + (1 - down) * b, False)
+
+        factor = HALF**-0.5
+        at = pl.multiple_of(a * rows, rows)
+        block = dkv_s[pl.ds(at, rows), :]
+        packed[a, :rows] = jnp.where(left, block * factor, block).astype(BF16)
+        top = dq_s[pl.ds(at, half), :]
+        low = dq_s[pl.ds(at + half, half), :]
+        packed[a, rows:] = (jnp.where(left_half, top, swap_halves(low)) * factor).astype(BF16)
+        index = xor8(a, me)
+
+        @pl.when(a == me)
+        def _():
+            pltpu.make_async_copy(packed.at[a], grads.at[me], x_recv.at[0]).start()
+
+        @pl.when(a != me)
+        def _():
+            remote(
+                packed.at[a],
+                grads.at[me],
+                x_send.at[index],
+                x_recv.at[index],
+                device(x, core, a // 2, a % 2),
+            ).start()
+
+    for _, finish, _ in sums:
+        finish(3)
+    sum_ou[...] = sums[0][2]()
+    sum_down[...] = sums[1][2]()
+    for index in range(blocks):
+        pltpu.make_async_copy(grads.at[0], grads.at[0], x_recv.at[index]).wait()
+        if index:
+            pltpu.make_async_copy(packed.at[0], packed.at[0], x_send.at[index]).wait()
+
+
+def backward(flags, got, do2, o, lse, acc_ou, acc_down, cid):
+    blocks = got.shape[0]
+    rows = got.shape[1] // 3 * 2
+    length = blocks * rows
+    lanes = 2 * HALF
+    vmem = pltpu.VMEM
+    dma = pltpu.SemaphoreType.DMA
+    ou, low = acc_ou.shape[3:], acc_down.shape[3:]
+    return pl.pallas_call(
+        backward_kernel,
+        out_shape=[
+            jax.ShapeDtypeStruct(got.shape, BF16),
+            jax.ShapeDtypeStruct(ou, F32),
+            jax.ShapeDtypeStruct(low, F32),
+        ],
+        in_specs=[SMEM_SPEC] + [VMEM_SPEC] * 6,
+        out_specs=[VMEM_SPEC] * 3,
+        scratch_shapes=[
+            vmem(got.shape, BF16),
+            vmem((length, lanes), BF16),
+            vmem((length, lanes), BF16),
+            vmem((length, lanes), BF16),
+            vmem((8, length), F32),
+            vmem((length, lanes), F32),
+            vmem((length, lanes), F32),
+        ]
+        + reduce_buffers(*ou, BF16)
+        + reduce_buffers(*low, BF16)
+        + [dma((2 * REDUCE_COPIES,)), dma((2 * REDUCE_COPIES,)), dma((blocks,)), dma((blocks,))],
+        compiler_params=params(cid),
+    )(flags, got, do2, o, lse, acc_ou, acc_down)
+
+
+def last_kernel(*refs):
+    grads, a1, tokens, dx, qkv_all, vec, sums_in = refs[:7]
+    out_ref, sum_qkv, sum_small = refs[7:10]
+    dqkv_s, sums, core_q, got_q, acc_q, core_small, got_small, acc_small = refs[10:18]
+    bufs_q = refs[18 : 18 + REDUCE_BUFFERS]
+    bufs_small = refs[18 + REDUCE_BUFFERS : 18 + 2 * REDUCE_BUFFERS]
+    r_send, r_recv, c_send, c_recv = refs[18 + 2 * REDUCE_BUFFERS :]
+    x, core, z, y = place()
+    oc = 1 - core
+    to_core = device(x, oc, z, y)
+    rows, width = tokens.shape
+    half = rows // 2
+    left_half = left_lanes(half)
+    left1 = left_lanes(1)
+    base = vec.shape[1] - 4 * width
+    greet(reduce_peers() + [to_core])
+    for j in range(HEADS // 2):
+        even, odd = grads[2 * j, rows:], grads[2 * j + 1, rows:]
+        at = 128 * j
+        dqkv_s[:half, at : at + 128] = jnp.where(left_half, even, swap_halves(odd))
+        dqkv_s[half:, at : at + 128] = jnp.where(left_half, swap_halves(even), odd)
+    for h in range(HEADS):
+        at = width + 128 * h
+        dqkv_s[:, at : at + 128] = grads[h, :rows]
+
+    def weight_grad(c, n):
+        at = pl.multiple_of((2 * n + c) * 128, 128)
+        return mm(a1[:, pl.ds(at, 128)], dqkv_s[...], TN).reshape(4, 2, 16, 3 * width)
+
+    for n in range(2):
+        core_q[n] = weight_grad(oc, n).astype(BF16)
+    over_q = remote(core_q, got_q, c_send.at[0], c_recv.at[0], to_core)
+    over_q.start()
+
+    sums[...] = sums_in[...]
+    dqkv = dqkv_s[...].astype(F32)
+    columns = jnp.sum(dqkv, axis=0, keepdims=True)
+    sums[0:1, :width] = columns[:, :width]
+    for j in range(HEADS // 2):
+        at = width + 256 * j
+        pair = jnp.where(
+            left1, swap_halves(columns[:, at : at + 128]), columns[:, at + 128 : at + 256]
+        )
+        sums[0:1, width + 128 * j : width + 128 * (j + 1)] = pair
+
+    w_qkv = qkv_all[:, :, :, :, :, : 3 * width].reshape(width, 3 * width)
+    dh = mm(dqkv_s[...], w_qkv, NT)
+    gain = vec[0:1, base : base + width]
+    value = tokens[...].astype(F32)
+    center = jnp.mean(value, axis=1, keepdims=True)
+    offset = value - center
+    spread = jnp.mean(offset * offset, axis=1, keepdims=True)
+    inverse = lax.rsqrt(spread + eps_norm)
+    norm = offset * inverse
+    sums[0:1, base : base + width] = jnp.sum(dh * norm, axis=0, keepdims=True)
+    sums[0:1, base + width : base + 2 * width] = jnp.sum(dh, axis=0, keepdims=True)
+
+    def small_block(a, b, c, d):
+        n = (a * 2 + b) * 8 + c * 2 + d
+        group = sums[0:1, pl.ds(pl.multiple_of(128 * n, 128), 128)]
+        pair = sums[0:1, pl.ds(pl.multiple_of(base + 128 * (n // 2), 128), 128)]
+        own = pair if d == 0 else swap_halves(pair)
+        return jnp.concatenate([group, own, jnp.zeros((6, 128), F32)], axis=0)
+
+    for a in range(2):
+        for c in range(4):
+            for d in range(2):
+                core_small[a, c, d] = small_block(a, oc, c, d)
+                acc_small[a, c, d] = small_block(a, core, c, d)
+    over_small = remote(core_small, got_small, c_send.at[1], c_recv.at[1], to_core)
+    over_small.start()
+    for n in range(2):
+        acc_q[n] = weight_grad(core, n)
+    over_q.wait()
+    acc_q[...] += got_q[...].astype(F32)
+    over_small.wait()
+    acc_small[...] += got_small[...]
+    parts = (
+        reducer(acc_q, bufs_q, r_send, r_recv, 0),
+        reducer(acc_small, bufs_small, r_send, r_recv, REDUCE_COPIES),
+    )
+    for launch, _, _ in parts:
+        launch(1)
+    e = dh * gain
+    mean_e = jnp.mean(e, axis=1, keepdims=True)
+    mean_en = jnp.mean(e * norm, axis=1, keepdims=True)
+    out_ref[...] = dx[...] + inverse * (e - mean_e - norm * mean_en)
+    for stage in (1, 2):
+        for _, finish, _ in parts:
+            finish(stage)
+        for launch, _, _ in parts:
+            launch(stage + 1)
+    for _, finish, _ in parts:
+        finish(3)
+    sum_qkv[...] = parts[0][2]()
+    sum_small[...] = parts[1][2]()
+
+
+def last(grads, a1, tokens, dx, qkv_all, vec, sums, cid):
+    rows, width = tokens.shape
+    vmem = pltpu.VMEM
+    dma = pltpu.SemaphoreType.DMA
+    part = (2, 4, 2, 16, 3 * width)
+    small = (2, 4, 2, 8, 128)
+    return pl.pallas_call(
+        last_kernel,
+        out_shape=[
+            jax.ShapeDtypeStruct((rows, width), F32),
+            jax.ShapeDtypeStruct((16, 3 * width), F32),
+            jax.ShapeDtypeStruct((8, 128), F32),
+        ],
+        in_specs=[VMEM_SPEC] * 7,
+        out_specs=[VMEM_SPEC] * 3,
+        scratch_shapes=[
+            vmem((rows, 3 * width), BF16),
+            vmem(sums.shape, F32),
+            vmem(part, BF16),
+            vmem(part, BF16),
+            vmem(part, F32),
+            vmem(small, F32),
+            vmem(small, F32),
+            vmem(small, F32),
+        ]
+        + reduce_buffers(16, 3 * width, BF16)
+        + reduce_buffers(8, 128, F32)
+        + [dma((2 * REDUCE_COPIES,)), dma((2 * REDUCE_COPIES,)), dma((2,)), dma((2,))],
+        compiler_params=params(cid),
+    )(grads, a1, tokens, dx, qkv_all, vec, sums)
+
+
+def flatten_kernel(sum_qkv, sum_ou, sum_down, sum_small, qkv_o, out_o, up_o, down_o, bias_o, norm_o):
+    groups = sum_down.shape[1] // 128
+    left = left_lanes(16)
+
+    def group(ref, j):
+        return ref[:, 128 * j : 128 * (j + 1)]
+
+    for j in range(groups):
+        qkv_o[pl.ds(j, 16, stride=3 * groups), :] = group(sum_qkv, j)
+        even, odd = group(sum_qkv, groups + 2 * j), group(sum_qkv, groups + 2 * j + 1)
+        qkv_o[pl.ds(groups + j, 16, stride=3 * groups), :] = jnp.where(
+            left, even, swap_halves(odd)
+        )
+        qkv_o[pl.ds(2 * groups + j, 16, stride=3 * groups), :] = jnp.where(
+            left, swap_halves(even), odd
+        )
+        out_o[pl.ds(j, 16, stride=groups), :] = group(sum_ou, j)
+        down_o[pl.ds(j, sum_down.shape[0], stride=groups), :] = group(sum_down, j)
+    ups = sum_ou.shape[1] // 128 - groups
+    for j in range(ups):
+        up_o[pl.ds(j, 16, stride=ups), :] = group(sum_ou, groups + j)
+    bias_o[...] = sum_small[0:1]
+    norm_o[...] = sum_small[1:2, : norm_o.shape[1]]
+
+
+def flatten(sum_qkv, sum_ou, sum_down, sum_small, norm_len):
+    width = sum_down.shape[1]
+    sizes = (
+        sum_qkv.size // 128,
+        width * 16 // 128,
+        (sum_ou.shape[1] - width) * 16 // 128,
+        sum_down.size // 128,
+    )
+    return pl.pallas_call(
+        flatten_kernel,
+        out_shape=[jax.ShapeDtypeStruct((n, 128), F32) for n in sizes]
+        + [jax.ShapeDtypeStruct((1, 128), F32), jax.ShapeDtypeStruct((1, norm_len), F32)],
+        in_specs=[VMEM_SPEC] * 4,
+        out_specs=[VMEM_SPEC] * 6,
+        compiler_params=params(),
+    )(sum_qkv, sum_ou, sum_down, sum_small)
+
+
+def fast_device(
+    tokens, piece_starts, qkv_weight, out_weight, up_weight, down_weight, biases, norms, cotangent
+):
+    seq_rows = tokens.shape[1]
+    length = seq_rows * HEADS
+    openings = jnp.arange(length // PIECE, dtype=jnp.int32) * PIECE
+    flags = jnp.any(openings[:, None] == piece_starts[0][None, :], axis=1).astype(jnp.int32)
+    bias_len = biases.shape[0]
+    norm_len = norms.shape[0]
+    small = jnp.concatenate([biases, norms, jnp.zeros((16 * 128 - bias_len - norm_len,), BF16)])
+    first_in, got, mix, o_heads, lse, vec, qkv_all, ou_all, down_all = forward(
+        flags,
+        tokens[0],
+        small.reshape(16, 128),
+        qkv_weight.reshape(-1, 128),
+        out_weight.reshape(-1, 128),
+        up_weight.reshape(-1, 128),
+        down_weight.reshape(-1, 128),
+        1,
+    )
+    output, grad_after, do2, acc_ou, acc_down, sums = middle(
+        tokens[0], cotangent[0], mix, vec, ou_all, down_all, 2
+    )
+    grads, sum_ou, sum_down = backward(flags, got, do2, o_heads, lse, acc_ou, acc_down, 3)
+    grad_tokens, sum_qkv, sum_small = last(
+        grads, first_in, tokens[0], grad_after, qkv_all, vec, sums, 4
+    )
+    flats = flatten(sum_qkv, sum_ou, sum_down, sum_small, norm_len)
+    return (output[None], grad_tokens[None]) + tuple(f.reshape(-1) for f in flats)
+
+
 def solution(mesh):
-    in_specs = (
-        P("dp", "ctx", None),
-        P("dp", None),
-        P(("dp", "ctx")),
-        P(("dp", "ctx")),
-        P(("dp", "ctx")),
-        P(("dp", "ctx")),
-        P(("dp", "ctx")),
-        P(("dp", "ctx")),
-        P("dp", "ctx", None),
-    )
-    out_specs = (
-        P("dp", "ctx", None),
-        P("dp", "ctx", None),
-        P(("dp", "ctx")),
-        P(("dp", "ctx")),
-        P(("dp", "ctx")),
-        P(("dp", "ctx")),
-        P(("dp", "ctx")),
-        P(("dp", "ctx")),
-    )
+    flat = P(("dp", "ctx"))
+    rows = P("dp", "ctx", None)
+    fast = mesh.shape["dp"] == 4 and mesh.shape["ctx"] == HEADS
     return jax.shard_map(
-        per_device, mesh=mesh, in_specs=in_specs, out_specs=out_specs, check_vma=False
-    )
+        fast_device if fast else general_device,
+        mesh=mesh,
+        in_specs=(rows, P("dp", None), flat, flat, flat, flat, flat, flat, rows),
+        out_specs=(rows, rows, flat, flat, flat, flat, flat, flat),
+        check_vma=False,
+    )

time: 1430 us -> 239 us (0.17); the launches traced: 1410 us -> 239 us
  matrix products: 510 us -> 0 us
  waiting for transfers between devices: 290 us -> 0 us
  blocking collectives: 245 us -> 0 us
  Pallas kernels: 0 us -> 233 us
  local copies, waits for them, and re-layouts: 180 us -> 3.78 us
  other arithmetic: 141 us -> 1.26 us
  loops' own time: 33.2 us -> 0 us
    dot_general x124 -> x0, matrix products: 510 us -> none  [the longest x16 91 us: key_terms(): jnp.einsum('hqk,qhd->hkd', dscores, query_block, preferred_element_type=j...]
    pallas_call x0 -> x5, Pallas kernels: none -> 233 us  [the longest x1 111 us: forward(): pl.pallas_call(forward_kernel, out_shape=[jax.ShapeDtypeStruct((rows, wid...]
    unnamed x9 -> x0, waiting for transfers between devices: 178 us -> none
    all_gather x3 -> x0, blocking collectives: 165 us -> none  [the longest x1 68.2 us: per_device(): lax.all_gather(out_weight, ('dp', 'ctx'), axis=0, tiled=True)]
    all_gather x7 -> x0, waiting for transfers between devices: 113 us -> none  [the longest x1 62.1 us: per_device(): lax.all_gather(key_rows, 'ctx', axis=0, tiled=True)]
    unnamed x2 -> x0, blocking collectives: 80.6 us -> none
    reduce_sum x27 -> x0, other arithmetic: 65.4 us -> none  [the longest x16 54.5 us: forward_one_block(): running_sum = running_sum * correction + jnp.sum(exp_scores, axis=-1)]
    dynamic_slice x48 -> x0, local copies, waits for them, and re-layouts: 38.4 us -> none  [forward_compute(): lax.scan(forward_one_block, state, (key_blocks, value_blocks, jnp.arange(...]
  transfers between devices with their start and end apart: 8 -> 0, of which waited for: 3 -> 0; matrix products, arithmetic and copies ran while one was open for 36% -> 0% of each run, Pallas kernels for 0% -> 0%
where the time goes in v1:
time: 239 us
  Pallas kernels  233 us (97%)
  local copies, waits for them, and re-layouts  3.78 us (2%)
    pallas_call x1, Pallas kernels, forward(): pl.pallas_call(forward_kernel, out_shape=[jax.ShapeDtypeStruct((rows, wid...  111 us
    pallas_call x1, Pallas kernels, backward(): pl.pallas_call(backward_kernel, out_shape=[jax.ShapeDtypeStruct(got.shape...  64 us
    pallas_call x1, Pallas kernels, middle(): pl.pallas_call(middle_kernel, out_shape=[jax.ShapeDtypeStruct((rows, widt...  30.4 us
    pallas_call x1, Pallas kernels, last(): pl.pallas_call(last_kernel, out_shape=[jax.ShapeDtypeStruct((rows, width)...  26.5 us

profile of v1, /device:TPU:0, one launch (start us, length us, event | category | flops | bytes accessed | tf_op | source)
XLA Modules:
  0.0 239.0 jit_solution(17253915162770470872)
XLA Ops:
  0.6 0.7 compare_reduce_fusion
  1.4 0.5 convert_element_type.3.flags.refs_0_
  1.9 2.0 concatenate.3
  3.9 110.5 %shard_map.152 = (bf16[512,512]{1,0:T(8,128)(2,1)}, bf16[8,768,128]{2,1,0:T(8,128)(2,1)}, bf16[8,256,128]{2,1,0:T(8,128)(2,1)}, f32[4096,128]{1,0:T(8,128)}, f32...) custom-call(s32[16]{0:T(128)} %convert_element_type.3.flags.refs_0_,, ...), custom_call_target="tpu_custom_call" | custom-call | tf_op jit(solution)/shard_map/pallas_call | solution.py:761
  114.4 30.4 %shard_map.153 = (bf16[512,512]{1,0:T(8,128)(2,1)}, f32[512,512]{1,0:T(8,128)}, bf16[8,256,128]{2,1,0:T(8,128)(2,1)}, f32[2,4,2,16,2560]{4,3,2,1,0:T(8,128)}, f3...) custom-call(bf16[512,512]{1,0:T(8,128)(2,1)} %bitcast.17, bf16[512,512]{1,0:T(8,128)(2,1)} %bitcast.20, ...), custom_call_target="tpu_custom_call" | custom-call | tf_op jit(solution)/shard_map/pallas_call | solution.py:985
  144.9 64.0 %shard_map.154 = (bf16[8,768,128]{2,1,0:T(8,128)(2,1)}, f32[16,2560]{1,0:T(8,128)}, f32[64,512]{1,0:T(8,128)}) custom-call(s32[16]{0:T(128)} %convert_element_type.3.flags.refs_0_, bf16[8,768,128]{2,1,0:T(8,128)(2,1)} %get-tuple-element.40.refs_1_, bf16[8,256,128]{2,1,0:T(8,128)(2,1)} %get-tuple-element.41.refs_2_, f32[4096,128]{1,0:T(8,128)} %get-tuple-element.42.refs_3_, ...), custom_call_target="tpu_custom_call" | custom-call | tf_op jit(solution)/shard_map/pallas_call | solution.py:1229
  208.9 0.0 copy-start.1
  208.9 26.5 %shard_map.155 = (f32[512,512]{1,0:T(8,128)}, f32[16,1536]{1,0:T(8,128)}, f32[8,128]{1,0:T(8,128)}) custom-call(bf16[8,768,128]{2,1,0:T(8,128)(2,1)} %get-tuple-element.46.refs_0_, bf16[512,512]{1,0:T(8,128)(2,1)} %get-tuple-element.47.refs_1_, bf16[512,512]{1,0:T(8,128)(2,1)} %bitcast.18, f32[512,512]{1,0:T(8,128)} %get-tuple-element.48.refs_3_, ...), custom_call_target="tpu_custom_call" | custom-call | tf_op jit(solution)/shard_map/pallas_call | solution.py:1358
  235.4 0.0 copy-start
  235.4 1.9 shard_map.156
  237.3 0.0 copy-done.1
  237.3 0.8 copy.19
  238.1 0.0 copy-done
  238.1 1.0 copy.20
  (2 shorter events, 0.0 us)
Async XLA Ops:
  208.9 28.4 %copy-start.1 = (bf16[512,512]{1,0:T(8,128)(2,1)S(1)}, bf16[512,512]{1,0:T(8,128)(2,1)}, u32[]{:S(2)}) copy-start(bf16[512,512]{1,0:T(8,128)(2,1)} %get-tuple-element.39) | copy-start | bytes 1572868
  235.4 2.7 %copy-start = (f32[512,512]{1,0:T(8,128)S(1)}, f32[512,512]{1,0:T(8,128)}, u32[]{:S(2)}) copy-start(f32[512,512]{1,0:T(8,128)} %get-tuple-element.51) | copy-start | bytes 3145732

commit v2 on v0

--- a/solution.py
+++ b/solution.py
@@ -1,6 +1,11 @@
+import math
+import types
+
 import jax
 import jax.numpy as jnp
 from jax import lax
+from jax.experimental import pallas as pl
+from jax.experimental.pallas import tpu as pltpu
 from jax.sharding import PartitionSpec as P
 
 HEADS = 8
@@ -124,7 +129,7 @@
     return (grad_keys, grad_values)
 
 
-def per_device(
+def general_device(
     tokens, piece_starts, qkv_weight, out_weight, up_weight, down_weight, biases, norms, cotangent
 ):
     model_width = tokens.shape[2]
@@ -380,28 +385,1233 @@
     return (output, grad_tokens, summed[0], summed[1], summed[2], summed[3], summed[4], summed[5])
 
 
+MESH = pl.DeviceIdType.MESH
+BF16 = jnp.bfloat16
+F32 = jnp.float32
+VMEM_SPEC = pl.BlockSpec(memory_space=pltpu.VMEM)
+SMEM_SPEC = pl.BlockSpec(memory_space=pltpu.SMEM)
+ANY_SPEC = pl.BlockSpec(memory_space=pl.ANY)
+HALF = 64
+NT = (((1,), (1,)), ((), ()))
+TN = (((0,), (0,)), ((), ()))
+VMEM_LIMIT = 60 << 20
+
+
+def params(cid=None):
+    if cid is None:
+        return pltpu.CompilerParams(vmem_limit_bytes=VMEM_LIMIT)
+    return pltpu.CompilerParams(
+        collective_id=cid, has_side_effects=True, vmem_limit_bytes=VMEM_LIMIT
+    )
+
+
+def place():
+    dp = lax.axis_index("dp")
+    ctx = lax.axis_index("ctx")
+    return dp // 2, dp % 2, ctx // 2, ctx % 2
+
+
+def device(x, core, z, y):
+    return (x * 2 + core, z * 2 + y)
+
+
+def greet(peers):
+    barrier = pltpu.get_barrier_semaphore()
+    for peer in peers:
+        pl.semaphore_signal(barrier, inc=1, device_id=peer, device_id_type=MESH)
+    pl.semaphore_wait(barrier, len(peers))
+
+
+def remote(src, dst, send, recv, peer):
+    return pltpu.make_async_remote_copy(
+        src_ref=src,
+        dst_ref=dst,
+        send_sem=send,
+        recv_sem=recv,
+        device_id=peer,
+        device_id_type=MESH,
+    )
+
+
+def mm(a, b, dims=None):
+    if dims is None:
+        return jnp.dot(a, b, preferred_element_type=F32)
+    return lax.dot_general(a, b, dims, preferred_element_type=F32)
+
+
+def swap_halves(v):
+    return jnp.concatenate([v[:, HALF:], v[:, :HALF]], axis=1)
+
+
+def left_lanes(rows):
+    return lax.broadcasted_iota(jnp.int32, (rows, 2 * HALF), 1) < HALF
+
+
+def diagonal_mask(size, flags, first, transposed):
+    row = lax.broadcasted_iota(jnp.int32, (size, size), 0)
+    col = lax.broadcasted_iota(jnp.int32, (size, size), 1)
+    key, query = (row, col) if transposed else (col, row)
+    allowed = key <= query
+    same = (key // PIECE) == (query // PIECE)
+    for t in range(size // PIECE):
+        inside = jnp.logical_and(same, (query // PIECE) == t)
+        allowed = jnp.logical_or(allowed, jnp.logical_and(inside, flags[first + t] > 0))
+    return allowed
+
+
+def xor8(a, b):
+    return (
+        (a // 4 + b // 4) % 2 * 4 + (a // 2 % 2 + b // 2 % 2) % 2 * 2 + (a % 2 + b % 2) % 2
+    )
+
+
+def unflatten(flat_ref, stage, rows, groups):
+    count = rows * groups
+    stage[pl.ds(0, count), :] = flat_ref[...].astype(F32)
+    return [stage[pl.ds(j, rows, stride=groups), :] for j in range(groups)]
+
+
+def reduce_buffers(rows, width, wire):
+    vmem = pltpu.VMEM
+    return [
+        vmem((2, 2, rows, width), wire),
+        vmem((2, 2, rows, width), wire),
+        vmem((2, 2, rows, width), wire),
+        vmem((2, 2, rows, width), wire),
+        vmem((2, 2, rows, width), wire),
+        vmem((2, 2, rows, width), wire),
+        vmem((4, rows, width), wire),
+        vmem((3, rows, width), wire),
+        vmem((4, rows, width), F32),
+    ]
+
+
+REDUCE_BUFFERS = 9
+REDUCE_COPIES = 7
+
+
+def reducer(acc, bufs, send, recv, first):
+    to_wire_x, from_x, to_wire_y, from_y, to_two, from_two, to_three, from_three, total = bufs
+    wire = to_wire_x.dtype
+    x, core, z, y = place()
+    ox, oy = 1 - x, 1 - y
+    to_x = device(ox, core, z, y)
+    to_y = device(x, core, z, oy)
+    others = [(z + j) % 4 for j in range(1, 4)]
+
+    def copies(stage):
+        def make(n, src, dst, peer):
+            return remote(src, dst, send.at[first + n], recv.at[first + n], peer)
+
+        if stage == 1:
+            return [make(0, to_wire_x, from_x, to_x), make(1, to_wire_y, from_y, to_y)]
+        if stage == 2:
+            return [
+                make(2, to_two.at[0], from_two.at[0], to_y),
+                make(3, to_two.at[1], from_two.at[1], to_x),
+            ]
+        return [
+            make(4 + j, to_three.at[other], from_three.at[j], device(x, core, other, y))
+            for j, other in enumerate(others)
+        ]
+
+    def launch(stage):
+        if stage == 1:
+            to_wire_x[...] = acc[ox, pl.ds(0, 2)].astype(wire)
+            for n in range(2):
+                to_wire_y[n] = acc[n, pl.ds(2, 2), oy].astype(wire)
+        elif stage == 2:
+            to_two[0] = (acc[x, pl.ds(0, 2), oy] + from_x[:, oy].astype(F32)).astype(wire)
+            to_two[1] = (acc[ox, pl.ds(2, 2), y] + from_y[ox].astype(F32)).astype(wire)
+        else:
+            low = acc[x, pl.ds(0, 2), y] + from_x[:, y].astype(F32) + from_two[0].astype(F32)
+            high = acc[x, pl.ds(2, 2), y] + from_y[x].astype(F32) + from_two[1].astype(F32)
+            total[pl.ds(0, 2)] = low
+            total[pl.ds(2, 2)] = high
+            to_three[pl.ds(0, 2)] = low.astype(wire)
+            to_three[pl.ds(2, 2)] = high.astype(wire)
+        for copy in copies(stage):
+            copy.start()
+
+    def finish(stage):
+        for copy in copies(stage):
+            copy.wait()
+
+    def result():
+        value = total[z]
+        for j in range(3):
+            value = value + from_three[j].astype(F32)
+        return value
+
+    return launch, finish, result
+
+
+def digits(values):
+    return sum(v * 4**n for n, v in enumerate(values))
+
+
+TILES = (
+    (
+        digits((0, 1, 1, 2, 2, 2, 3, 3, 3, 3)),
+        digits((0, 1, 0, 0, 1, 2, 0, 1, 2, 3)),
+        digits((1, 0, 1, 0, 0, 1, 0, 0, 0, 1)),
+    ),
+    (
+        digits((2, 3, 3, 2, 3, 0, 2, 3, 1, 1)),
+        digits((2, 3, 2, 0, 0, 0, 1, 1, 0, 1)),
+        digits((0, 0, 0, 0, 0, 1, 1, 1, 0, 1)),
+    ),
+)
+
+
+def forward_phase(r):
+    flags = r.flags
+    tokens = r.tokens
+    small = r.small
+    qkv_flat = r.qkv_flat
+    out_flat = r.out_flat
+    up_flat = r.up_flat
+    down_flat = r.down_flat
+    a1_ref = r.a1
+    got = r.got
+    mix = r.mix
+    o_ref = r.o_heads
+    lse_ref = r.lse
+    vec_ref = r.vec
+    qkv_all = r.qkv_all
+    ou_all = r.ou_all
+    down_all = r.down_all
+    stage = r.stage
+    qkv_own = r.qkv_own
+    ou_own = r.ou_own
+    down_own = r.down_own
+    norm_s = r.n2_s
+    packed = r.packed
+    q_s = r.q_s
+    k_s = r.k_s
+    v_s = r.v_s
+    m_s = r.m_s
+    acc_s = r.acc_s
+    o2_s = r.o2_s
+    g_own = r.g_own
+    g_send = r.g_send
+    g_recv = r.g_recv
+    f_send = r.f_send
+    f_recv = r.f_recv
+    x_send = r.x_send
+    x_recv = r.x_recv
+    o_send = r.o_send
+    o_recv = r.o_recv
+    x, core, z, y = place()
+    ox, oc, oy = 1 - x, 1 - core, 1 - y
+    me = z * 2 + y
+    width = tokens.shape[1]
+    rows = tokens.shape[0]
+    half = rows // 2
+    tile = 2 * rows
+    groups = width // 128
+    group = 3 * width // 2
+    scale = math.log2(math.e) * HALF**-0.5
+    left = left_lanes(rows)
+    left_half = left_lanes(half)
+    to_x = device(ox, core, z, y)
+    to_y = device(x, core, z, oy)
+    to_core = device(x, oc, z, y)
+    others = [(z + j) % 4 for j in range(1, 4)]
+
+    qkv = unflatten(qkv_flat, stage, 16, 3 * groups)
+    left16 = left_lanes(16)
+    for j in range(groups):
+        k_pair, v_pair = qkv[groups + j], qkv[2 * groups + j]
+        at = (j // 2) * group + (j % 2) * 128
+        qkv_own[:, at : at + 128] = qkv[j].astype(BF16)
+        at = (j // 2) * group + 256 + (j % 2) * 256
+        qkv_own[:, at : at + 128] = jnp.where(left16, k_pair, swap_halves(v_pair)).astype(BF16)
+        at += 128
+        qkv_own[:, at : at + 128] = jnp.where(left16, swap_halves(k_pair), v_pair).astype(BF16)
+    qkv_own[:, 3 * width :] = small[...]
+    greet(
+        [device(x, core, (z + c) % 4, (y + d) % 2) for c in range(4) for d in range(2)][1:]
+        + [to_x, to_core]
+    )
+    arrays = ((qkv_own, qkv_all), (ou_own, ou_all), (down_own, down_all))
+
+    def moves(phase, a):
+        own, full = arrays[a]
+        if phase == 1:
+            mine = full.at[x, core, z, y]
+            return [(own, mine, device(x, core, o, y), j) for j, o in enumerate(others)]
+        if phase == 2:
+            part = full.at[x, core, :, y]
+            return [(part, part, to_x, 3), (part, part, to_y, 4), (part, part, to_core, 5)]
+        if phase == 3:
+            low = full.at[x, core, pl.ds(0, 2), oy]
+            high = full.at[ox, core, pl.ds(2, 2), y]
+            from_x = full.at[ox, core, :, y]
+            from_y = full.at[x, core, :, oy]
+            return [
+                (low, low, to_x, 6),
+                (high, high, to_y, 7),
+                (from_x, from_x, to_core, 8),
+                (from_y, from_y, to_core, 9),
+            ]
+        part = full.at[ox, core, :, oy]
+        return [(part, part, to_core, 10)]
+
+    def phase_copies(phase, a):
+        copies = [
+            remote(src, dst, g_send.at[a * 11 + n], g_recv.at[a * 11 + n], peer)
+            for src, dst, peer, n in moves(phase, a)
+        ]
+        if phase == 1:
+            own, full = arrays[a]
+            copies.append(pltpu.make_async_copy(own, full.at[x, core, z, y], g_own.at[a]))
+        return copies
+
+    def launch(phase, a):
+        for copy in phase_copies(phase, a):
+            copy.start()
+
+    def finish(phase, a):
+        for copy in phase_copies(phase, a):
+            copy.wait()
+
+    first = arrays[0][1]
+
+    def hop(src, dst, peer, n):
+        return remote(src, dst, f_send.at[n], f_recv.at[n], peer)
+
+    def to_xy(c):
+        part = first.at[x, core, c, y]
+        return hop(part, part, to_x, 4 + c), hop(part, part, to_y, 8 + c)
+
+    def corner(c, over_x):
+        if over_x:
+            part = first.at[x, core, c, oy]
+            return hop(part, part, to_x, 12 + c)
+        part = first.at[ox, core, c, y]
+        return hop(part, part, to_y, 12 + c)
+
+    def to_sibling(n):
+        part = (
+            first.at[x, core, :, y],
+            first.at[ox, core, :, y],
+            first.at[x, core, :, oy],
+            first.at[ox, core, :, oy],
+        )[n]
+        return hop(part, part, to_core, 16 + n)
+
+    own_first = pltpu.make_async_copy(qkv_own, first.at[x, core, z, y], g_own.at[0])
+    own_first.start()
+    along = [
+        hop(qkv_own, first.at[x, core, z, y], device(x, core, other, y), n)
+        for n, other in enumerate(others)
+    ]
+    own_xy = [
+        hop(qkv_own, first.at[x, core, z, y], to_x, 4 + z),
+        hop(qkv_own, first.at[x, core, z, y], to_y, 8 + z),
+    ]
+    for copy in along + own_xy:
+        copy.start()
+    out_parts = unflatten(out_flat, stage, 16, groups)
+    for j in range(groups):
+        ou_own[:, 128 * j : 128 * (j + 1)] = out_parts[j].astype(BF16)
+    up_groups = up_flat.shape[0] // 16
+    up_parts = unflatten(up_flat, stage, 16, up_groups)
+    for j in range(up_groups):
+        at = width + 128 * j
+        ou_own[:, at : at + 128] = up_parts[j].astype(BF16)
+    down_rows = down_flat.shape[0] // groups
+    down_parts = unflatten(down_flat, stage, down_rows, groups)
+    for j in range(groups):
+        down_own[:, 128 * j : 128 * (j + 1)] = down_parts[j].astype(BF16)
+    launch(1, 1)
+    launch(1, 2)
+    own_first.wait()
+    for n in range(3):
+        along[n].wait_recv()
+        for copy in to_xy((z + 3 - n) % 4):
+            copy.start()
+    to_sibling(0).start()
+    value = tokens[...].astype(F32)
+    center = jnp.mean(value, axis=1, keepdims=True)
+    offset = value - center
+    spread = jnp.mean(offset * offset, axis=1, keepdims=True)
+    norm_s[...] = offset * lax.rsqrt(spread + eps_norm)
+    for c in [z] + others:
+        over_x, over_y = to_xy(c)
+        over_x.wait_recv()
+        over_y.wait_recv()
+
+        @pl.when(c < 2)
+        def _():
+            corner(c, True).start()
+
+        @pl.when(c >= 2)
+        def _():
+            corner(c, False).start()
+
+    to_sibling(1).start()
+    to_sibling(2).start()
+    for c in range(4):
+        corner(c, c < 2).wait()
+    to_sibling(3).start()
+    for n in range(4):
+        to_sibling(n).wait()
+    for copy in along:
+        copy.wait_send()
+    for c in range(4):
+        for copy in to_xy(c):
+            copy.wait_send()
+
+    vec_ref[...] = jnp.zeros_like(vec_ref)
+    devices = [(a, b, c, d) for a in range(2) for b in range(2) for c in range(4) for d in range(2)]
+    base = 128 * len(devices)
+
+    def bias_rows(begin, end):
+        for n in range(begin, end):
+            piece = first[devices[n] + (slice(None), pl.ds(3 * width, 128))].astype(F32)
+            vec_ref[0:1, 128 * n : 128 * (n + 1)] = piece[0:1]
+
+    def norm_rows(begin, end):
+        for n in range(begin, end):
+            pair = [
+                first[devices[2 * n + d] + (slice(None), pl.ds(3 * width, 128))].astype(F32)
+                for d in range(2)
+            ]
+            joined = jnp.concatenate([pair[0][1:2, :HALF], pair[1][1:2, :HALF]], axis=1)
+            vec_ref[0:1, base + 128 * n : base + 128 * (n + 1)] = joined
+
+    bias_rows(0, 2 * groups)
+    norm_rows(0, 2 * groups)
+    gain = vec_ref[0:1, base : base + width]
+    shift = vec_ref[0:1, base + width : base + 2 * width]
+    a1_ref[...] = (norm_s[...] * gain + shift).astype(BF16)
+
+    def part_of(is_query):
+        return pl.ds(rows, half) if is_query else pl.ds(0, rows)
+
+    def send_part(tz, mark, is_query):
+        for step in range(2):
+            ty = (y + step) % 2
+            index = mark + step
+            src = packed.at[2 * tz + ty, part_of(is_query)]
+            dst = got.at[me, part_of(is_query)]
+            n = index + 8 * is_query
+            if index == 0:
+                pltpu.make_async_copy(src, dst, x_recv.at[n]).start()
+            else:
+                remote(src, dst, x_send.at[n], x_recv.at[n], device(x, core, tz, ty)).start()
+
+    hz = z // 2
+    order = (hz * 2 + 1 - z % 2, z, (1 - hz) * 2 + z % 2, (1 - hz) * 2 + 1 - z % 2)
+    marks = (2, 0, 4, 6)
+    left1 = left_lanes(1)
+    for tz, mark in zip(order, marks):
+        a1 = a1_ref[...]
+        at = pl.multiple_of(tz // 2 * group + tz % 2 * 128, 128)
+        w_q = qkv_all[:, :, :, :, :, pl.ds(at, 128)].reshape(width, 128)
+        q = (mm(a1, w_q) + vec_ref[0:1, pl.ds(pl.multiple_of(128 * tz, 128), 128)]).astype(BF16)
+        at_kv = pl.multiple_of(tz // 2 * group + 256 + tz % 2 * 256, 128)
+        w_kv = qkv_all[:, :, :, :, :, pl.ds(at_kv, 256)].reshape(width, 256)
+        bias = vec_ref[0:1, pl.ds(pl.multiple_of(width + 128 * tz, 128), 128)]
+        kv = mm(a1, w_kv)
+        even = kv[:, :128] + jnp.where(left1, 0.0, swap_halves(bias))
+        odd = kv[:, 128:] + jnp.where(left1, 0.0, bias)
+        packed[2 * tz, :rows] = even.astype(BF16)
+        packed[2 * tz + 1, :rows] = odd.astype(BF16)
+        top, low = q[:half], q[half:]
+        packed[2 * tz, rows:] = jnp.where(left_half, top, swap_halves(low))
+        packed[2 * tz + 1, rows:] = jnp.where(left_half, swap_halves(top), low)
+        if mark < 4:
+            send_part(tz, mark, False)
+            send_part(tz, mark, True)
+
+    def send_cross():
+        def send_all(is_query):
+            for tz, mark in zip(order[2:], marks[2:]):
+                send_part(tz, mark, is_query)
+
+        pl.when(hz == 1)(lambda: send_all(True))
+        send_all(False)
+        pl.when(hz == 0)(lambda: send_all(True))
+
+    pl.when(z % 2 == 0)(send_cross)
+    finish(1, 1)
+    finish(1, 2)
+    launch(2, 1)
+    launch(2, 2)
+    bias_rows(2 * groups, len(devices))
+    norm_rows(2 * groups, len(devices) // 2)
+
+    def block_wait(sems, index, view):
+        pltpu.make_async_copy(view, view, sems.at[index]).wait()
+
+    def arrive(part, is_query):
+        for t in range(2):
+            b = 2 * part + t
+            block_wait(x_recv, xor8(b, me) + 8 * is_query, got.at[b, part_of(is_query)])
+            at = pl.multiple_of(b * rows, rows)
+            if is_query:
+                both = got[b, rows:]
+                q_s[pl.ds(at, half), :] = jnp.where(left_half, both, 0).astype(BF16)
+                q_s[pl.ds(at + half, half), :] = jnp.where(
+                    left_half, swap_halves(both), 0
+                ).astype(BF16)
+            else:
+                pair = got[b, :rows]
+                k_s[pl.ds(at, rows), :] = jnp.where(left, pair, 0).astype(BF16)
+                v_s[pl.ds(at, rows), :] = jnp.where(left, 1, pair).astype(BF16)
+
+    low = 1 - hz
+    queries = low * TILES[0][0] + hz * TILES[1][0]
+    keys = low * TILES[0][1] + hz * TILES[1][1]
+    ends = low * TILES[0][2] + hz * TILES[1][2]
+    m_s[...] = jnp.full(m_s.shape, masked_score, F32)
+    acc_s[...] = jnp.zeros(acc_s.shape, F32)
+    for n in range(2):
+        arrive(2 * hz + n, False)
+        arrive(2 * hz + n, True)
+
+    def step(n, carry):
+        q_left, k_left, e_left = carry
+        i, j, done = q_left % 4, k_left % 4, e_left % 4
+
+        @pl.when(n == 3)
+        def _():
+            pl.when(z % 2 == 1)(send_cross)
+            for a in (1, 2):
+                finish(2, a)
+                launch(3, a)
+
+        @pl.when(n == 6)
+        def _():
+            for a in (1, 2):
+                finish(3, a)
+                launch(4, a)
+
+        for when, part, is_query in ((3, 2, 1), (5, 2, 0), (6, 3, 1), (9, 3, 0)):
+            pl.when(n == when + 16 * hz)(lambda: arrive(part, is_query))
+        for when, part, is_query in ((3, 0, 0), (5, 0, 1), (6, 1, 0), (8, 1, 1)):
+            pl.when(n == when + 16 * low)(lambda: arrive(part, is_query))
+
+        at = pl.multiple_of(i * tile, tile)
+        begin = pl.multiple_of(j * tile, tile)
+
+        def update(diagonal):
+            s = mm(q_s[pl.ds(at, tile), :], k_s[pl.ds(begin, tile), :], NT)
+            if diagonal:
+                allowed = diagonal_mask(tile, flags, i * (tile // PIECE), False)
+                s = jnp.where(allowed, s, masked_score)
+            old = m_s[pl.ds(at, tile), :]
+            new = jnp.maximum(old, jnp.max(s, axis=1, keepdims=True) * scale)
+            p = jnp.exp2(s * scale - new[:, :1])
+            m_s[pl.ds(at, tile), :] = new
+            acc_s[pl.ds(at, tile), :] = acc_s[pl.ds(at, tile), :] * jnp.exp2(old - new) + mm(
+                p.astype(BF16), v_s[pl.ds(begin, tile), :]
+            )
+
+        pl.when(i == j)(lambda: update(True))
+        pl.when(i != j)(lambda: update(False))
+
+        @pl.when(done == 1)
+        def _():
+            acc = acc_s[pl.ds(at, tile), :]
+            total = jnp.broadcast_to(acc[:, :1], acc.shape)
+            o = acc / total
+            o_ref[pl.ds(at, tile), :] = o
+            lse = m_s[pl.ds(at, tile), :] + jnp.log2(total)
+            lse_ref[:, pl.ds(at, tile)] = jnp.transpose(lse)[:8]
+            for t in range(2):
+                b = 2 * i + t
+                top = o[t * rows : t * rows + half]
+                bottom = o[t * rows + half : (t + 1) * rows]
+                o2_s[b] = jnp.where(left_half, swap_halves(top), bottom).astype(BF16)
+                index = xor8(b, me)
+
+                @pl.when(b == me)
+                def _():
+                    pltpu.make_async_copy(o2_s.at[b], mix.at[me], o_recv.at[0]).start()
+
+                @pl.when(b != me)
+                def _():
+                    remote(
+                        o2_s.at[b],
+                        mix.at[me],
+                        o_send.at[index],
+                        o_recv.at[index],
+                        device(x, core, i, t),
+                    ).start()
+
+        return q_left // 4, k_left // 4, e_left // 4
+
+    lax.fori_loop(0, 10, step, (queries, keys, ends))
+    for a in (1, 2):
+        finish(4, a)
+    for index in range(8):
+        block_wait(o_recv, index, mix.at[0])
+        if index:
+            block_wait(x_send, index, packed.at[0, part_of(False)])
+            block_wait(x_send, index + 8, packed.at[0, part_of(True)])
+            block_wait(o_send, index, o2_s.at[0])
+
+
+def middle_phase(r):
+    tokens = r.tokens
+    cot = r.cot
+    mix = r.mix
+    vec = r.vec
+    ou_all = r.ou_all
+    down_all = r.down_all
+    out_ref = r.out_ref
+    dx_ref = r.n2_s
+    do2_ref = r.do2
+    acc_ou = r.acc_ou
+    acc_down = r.acc_down
+    sums_ref = r.sums
+    o_s = r.o_s
+    x1_s = r.x1_s
+    n2_s = r.n2_s
+    a2_s = r.a2_s
+    gl_s = r.gl_s
+    du_s = r.du_s
+    dh_s = r.dh_s
+    da_s = r.da_s
+    r_s = r.r_s
+    send2 = r.o2_s
+    core_ou = r.core_ou
+    core_down = r.core_down
+    got_ou = r.got_ou
+    got_down = r.got_down
+    x_send = r.d_send
+    x_recv = r.d_recv
+    c_send = r.c_send
+    c_recv = r.c_recv
+    x, core, z, y = place()
+    oc, oy = 1 - core, 1 - y
+    me = z * 2 + y
+    rows, width = tokens.shape
+    half = rows // 2
+    hidden = ou_all.shape[-1] - width
+    left_half = left_lanes(half)
+    to_core = device(x, oc, z, y)
+    bias_o = vec[0:1, 2 * width : 3 * width]
+    bias_down = vec[0:1, 3 * width + hidden : 4 * width + hidden]
+    base = 4 * width + hidden
+    gain = vec[0:1, base + 2 * width : base + 3 * width]
+    shift = vec[0:1, base + 3 * width : base + 4 * width]
+
+    for j in range(HEADS // 2):
+        even, odd = mix[2 * j], mix[2 * j + 1]
+        at = 128 * j
+        o_s[:half, at : at + 128] = jnp.where(left_half, even, swap_halves(odd))
+        o_s[half:, at : at + 128] = jnp.where(left_half, swap_halves(even), odd)
+    w_out = ou_all[:, :, :, :, :, :width].reshape(width, width)
+    x1 = tokens[...].astype(F32) + mm(o_s[...], w_out) + bias_o
+    x1_s[...] = x1
+    center = jnp.mean(x1, axis=1, keepdims=True)
+    offset = x1 - center
+    spread = jnp.mean(offset * offset, axis=1, keepdims=True)
+    inverse = lax.rsqrt(spread + eps_norm)
+    r_s[...] = jnp.broadcast_to(inverse, r_s.shape)
+    n2 = offset * inverse
+    n2_s[...] = n2
+    a2_s[...] = (n2 * gain + shift).astype(BF16)
+    sums_ref[...] = jnp.zeros_like(sums_ref)
+
+    @pl.loop(0, hidden // width)
+    def _(j):
+        at = pl.multiple_of(j * width, width)
+        w_up = ou_all[:, :, :, :, :, pl.ds(pl.multiple_of(width + at, width), width)].reshape(
+            width, width
+        )
+        b_up = vec[0:1, pl.ds(pl.multiple_of(3 * width + at, width), width)]
+        w_down = down_all[j // 2, j % 2].reshape(width, width)
+        u = mm(a2_s[...], w_up) + b_up
+        phi = 0.5 * (1.0 + lax.erf(u * (0.5**0.5)))
+        slope = phi + u * jnp.exp(-0.5 * u * u) * (1.0 / math.sqrt(2.0 * math.pi))
+        gl_s[:, pl.ds(at, width)] = (u * phi).astype(BF16)
+        grad = mm(cot[...], w_down, NT)
+        du = (grad * slope).astype(BF16)
+        du_s[:, pl.ds(at, width)] = du
+        sums_ref[0:1, pl.ds(pl.multiple_of(3 * width + at, width), width)] = jnp.sum(
+            du.astype(F32), axis=0, keepdims=True
+        )
+        part = mm(du, w_up, NT)
+
+        @pl.when(j == 0)
+        def _():
+            dh_s[...] = part
+
+        @pl.when(j > 0)
+        def _():
+            dh_s[...] += part
+
+    dh2 = dh_s[...]
+    n2 = n2_s[...]
+    sums_ref[0:1, base + 2 * width : base + 3 * width] = jnp.sum(dh2 * n2, axis=0, keepdims=True)
+    sums_ref[0:1, base + 3 * width : base + 4 * width] = jnp.sum(dh2, axis=0, keepdims=True)
+    e = dh2 * gain
+    mean_e = jnp.mean(e, axis=1, keepdims=True)
+    mean_en = jnp.mean(e * n2, axis=1, keepdims=True)
+    dx = cot[...].astype(F32) + r_s[:, :1] * (e - mean_e - n2 * mean_en)
+    dx_ref[...] = dx
+    da = dx.astype(BF16)
+    da_s[...] = da
+    w_out = ou_all[:, :, :, :, :, :width].reshape(width, width)
+    grad_o = mm(da, w_out, NT).astype(BF16)
+    for j in range(HEADS // 2):
+        group = grad_o[:, 128 * j : 128 * (j + 1)]
+        top, low = group[:half], group[half:]
+        send2[2 * j] = jnp.where(left_half, top, swap_halves(low))
+        send2[2 * j + 1] = jnp.where(left_half, swap_halves(top), low)
+    hz = z // 2
+    order = ((1 - hz) * 2 + z % 2, (1 - hz) * 2 + 1 - z % 2, hz * 2 + 1 - z % 2, z)
+    for tz, mark in zip(order, (4, 6, 2, 0)):
+        for step in range(2):
+            ty = (y + step) % 2
+            index = mark + step
+            src = send2.at[2 * tz + ty]
+            if index == 0:
+                pltpu.make_async_copy(src, do2_ref.at[me], x_recv.at[0]).start()
+            else:
+                remote(
+                    src,
+                    do2_ref.at[me],
+                    x_send.at[index],
+                    x_recv.at[index],
+                    device(x, core, tz, ty),
+                ).start()
+
+    def grads(c, n):
+        dp = 2 * n + c
+        at = pl.multiple_of(dp * 128, 128)
+        down_at = pl.multiple_of(dp * width, width)
+        d_down = mm(gl_s[:, pl.ds(down_at, width)], cot[...], TN)
+        d_up = mm(a2_s[:, pl.ds(at, 128)], du_s[...], TN)
+        d_out = mm(o_s[:, pl.ds(at, 128)], da_s[...], TN)
+        return (
+            d_down.reshape(4, 2, width // 8, width),
+            d_up.reshape(4, 2, 16, hidden),
+            d_out.reshape(4, 2, 16, width),
+        )
+
+    for n in range(2):
+        d_down, d_up, d_out = grads(oc, n)
+        core_down[n] = d_down.astype(BF16)
+        core_ou[n, :, :, :, width:] = d_up.astype(BF16)
+        core_ou[n, :, :, :, :width] = d_out.astype(BF16)
+    to_ou = remote(core_ou, got_ou, c_send.at[0], c_recv.at[0], to_core)
+    to_down = remote(core_down, got_down, c_send.at[1], c_recv.at[1], to_core)
+    to_ou.start()
+    to_down.start()
+    sums_ref[0:1, 2 * width : 3 * width] = jnp.sum(da_s[...].astype(F32), axis=0, keepdims=True)
+    sums_ref[0:1, 3 * width + hidden : 4 * width + hidden] = jnp.sum(
+        cot[...].astype(F32), axis=0, keepdims=True
+    )
+    result = x1_s[...] + mm(gl_s[...], down_all[...].reshape(hidden, width)) + bias_down
+    out_ref[...] = result.astype(BF16)
+    for n in range(2):
+        d_down, d_up, d_out = grads(core, n)
+        acc_down[n] = d_down
+        acc_ou[n, :, :, :, width:] = d_up
+        acc_ou[n, :, :, :, :width] = d_out
+    to_ou.wait()
+    to_down.wait()
+    acc_ou[...] += got_ou[...].astype(F32)
+    acc_down[...] += got_down[...].astype(F32)
+
+
+def lanes_of(ref, r, g):
+    group = r.tokens.shape[1] * 3 // 2
+    return ref.at[:, :, :, :, pl.ds(pl.multiple_of(g * group, 128), group)]
+
+
+def reducer_of(r, name, first, at=None):
+    bufs = [getattr(r, f"{name}{n}") for n in range(REDUCE_BUFFERS)]
+    if at is not None:
+        return reducer(lanes_of(r.acc_ou, r, at), [b.at[at] for b in bufs], r.r_send, r.r_recv, first)
+    acc = getattr(r, f"acc_{name}")
+    return reducer(acc, bufs, r.r_send, r.r_recv, first)
+
+
+def backward_phase(r):
+    got, do2, o_heads, lse, grads, packed = r.got, r.do2, r.o_heads, r.lse, r.grads, r.packed
+    qd_s, k_s, v_s, delta_s, dq_s, dkv_s = r.q_s, r.k_s, r.v_s, r.delta_s, r.acc_s, r.m_s
+    flags = r.flags
+    x, core, z, y = place()
+    me = z * 2 + y
+    hz = z // 2
+    low = 1 - hz
+    blocks = got.shape[0]
+    rows = got.shape[1] // 3 * 2
+    half = rows // 2
+    quarter = blocks // 2
+    scale = math.log2(math.e) * HALF**-0.5
+    factor = HALF**-0.5
+    left = left_lanes(rows)
+    left_half = left_lanes(half)
+    sums = (reducer_of(r, "ou", 0), reducer_of(r, "down", REDUCE_COPIES))
+    for launch, _, _ in sums:
+        launch(1)
+
+    def enter(b):
+        at = pl.multiple_of(b * rows, rows)
+        pltpu.make_async_copy(do2.at[b], do2.at[b], r.d_recv.at[xor8(b, me)]).wait()
+        v_s[pl.ds(at, rows), :] = jnp.where(left, 0, v_s[pl.ds(at, rows), :]).astype(BF16)
+        grad = do2[b]
+        for part, begin in ((swap_halves(grad), 0), (grad, half)):
+            rows_at = pl.ds(at + begin, half)
+            qd_s[rows_at, :] = jnp.where(left_half, qd_s[rows_at, :], part)
+            product = jnp.where(left_half, 0.0, part.astype(F32) * o_heads[rows_at, :])
+            delta = jnp.sum(jnp.transpose(product), axis=0, keepdims=True)
+            delta_s[:, rows_at] = jnp.broadcast_to(delta, (8, half))
+        dq_s[pl.ds(at, rows), :] = jnp.zeros((rows, 2 * HALF), F32)
+        dkv_s[pl.ds(at, rows), :] = jnp.zeros((rows, 2 * HALF), F32)
+
+    def tile(kj, qi, diagonal):
+        k0 = pl.multiple_of(kj * rows, rows)
+        q0 = pl.multiple_of(qi * rows, rows)
+        k = k_s[pl.ds(k0, rows), :]
+        v = v_s[pl.ds(k0, rows), :]
+        qd = qd_s[pl.ds(q0, rows), :]
+        scores = mm(k, qd, NT)
+        dprobs = mm(v, qd, NT)
+        p = jnp.exp2(scores * scale - lse[:1, pl.ds(q0, rows)])
+        if diagonal:
+            allowed = diagonal_mask(rows, flags, kj * (rows // PIECE), True)
+            p = jnp.where(allowed, p, 0.0)
+        ds = (p * (dprobs - delta_s[:1, pl.ds(q0, rows)])).astype(BF16)
+        dkv_s[pl.ds(k0, rows), :] += jnp.where(left, mm(ds, qd), mm(p.astype(BF16), qd))
+        dq_s[pl.ds(q0, rows), :] += mm(ds, k, TN)
+
+    def part_of(is_query):
+        return pl.ds(rows, half) if is_query else pl.ds(0, rows)
+
+    def leave(a, is_query):
+        at = pl.multiple_of(a * rows, rows)
+        if is_query:
+            top = dq_s[pl.ds(at, half), :]
+            bottom = dq_s[pl.ds(at + half, half), :]
+            packed[a, rows:] = (
+                jnp.where(left_half, top, swap_halves(bottom)) * factor
+            ).astype(BF16)
+        else:
+            block = dkv_s[pl.ds(at, rows), :]
+            packed[a, :rows] = jnp.where(left, block * factor, block).astype(BF16)
+        index = xor8(a, me) + 8 * is_query
+        src = packed.at[a, part_of(is_query)]
+        dst = grads.at[me, part_of(is_query)]
+
+        @pl.when(a == me)
+        def _():
+            pltpu.make_async_copy(src, dst, r.b_recv.at[index]).start()
+
+        @pl.when(a != me)
+        def _():
+            remote(
+                src, dst, r.b_send.at[index], r.b_recv.at[index], device(x, core, a // 2, a % 2)
+            ).start()
+
+    for n in range(quarter):
+        enter(hz * quarter + n)
+
+    @pl.loop(0, 12)
+    def _(row):
+        seg = (row + 3) // 4
+        last = seg // 3
+        first = (3 - seg) // 3
+        square = seg // 2 - last
+        cross = seg % 2 - last
+        own = first + last
+        i = (row + 3) % 4 + last - 3 * first
+
+        @pl.when(row == 1)
+        def _():
+            for n in range(quarter):
+                enter(low * quarter + n)
+
+        for stage, step in ((1, 4), (2, 6)):
+
+            @pl.when(row == step)
+            def _():
+                for _, finish, _ in sums:
+                    finish(stage)
+                for launch, _, _ in sums:
+                    launch(stage + 1)
+
+        a_low = own * (3 - i) + (1 - own) * (7 - i)
+        a_high = own * (4 + i) + (1 - own) * i
+        a = low * a_low + hz * a_high
+        count = own * (3 - i) + cross * i + square * 4
+
+        @pl.when(square == 0)
+        def _():
+            tile(a, a, True)
+
+        @pl.loop(0, count)
+        def _(u):
+            k_low = (own + square) * u + cross * a_low
+            q_low = (own + square) * a_low + cross * (7 - u)
+            k_high = (own + square) * a_high + cross * u
+            q_high = own * (5 + i + u) + cross * a_high + square * (4 + u)
+            tile(low * k_low + hz * k_high, low * q_low + hz * q_high, False)
+
+        @pl.when(cross * hz + square * low + last > 0)
+        def _():
+            leave(a, 1)
+
+        @pl.when(cross * low + square * hz + last > 0)
+        def _():
+            leave(a, 0)
+
+        @pl.when(row == 8)
+        def _():
+            begin = low * 3 + hz * 4
+            leave(begin, 1)
+            leave(begin, 0)
+
+
+def last_phase(r):
+    grads, a1, tokens, dx, qkv_all, vec, sums = (
+        r.grads,
+        r.a1,
+        r.tokens,
+        r.n2_s,
+        r.qkv_all,
+        r.vec,
+        r.sums,
+    )
+    dqkv_s, got_q = r.gl_s, r.got_q
+    core_small, got_small, acc_small = r.core_small, r.got_small, r.acc_small
+    x, core, z, y = place()
+    me = z * 2 + y
+    hz = z // 2
+    oc = 1 - core
+    to_core = device(x, oc, z, y)
+    rows, width = tokens.shape
+    half = rows // 2
+    group = 3 * width // 2
+    left_half = left_lanes(half)
+    left1 = left_lanes(1)
+    base = vec.shape[1] - 4 * width
+
+    def columns_of(g):
+        return pl.ds(pl.multiple_of(g * group, 128), group)
+
+    def enter(g):
+        for n in range(HEADS // 2):
+            h = g * (HEADS // 2) + n
+            for is_query in range(2):
+                view = grads.at[h, pl.ds(rows, half) if is_query else pl.ds(0, rows)]
+                pltpu.make_async_copy(view, view, r.b_recv.at[xor8(h, me) + 8 * is_query]).wait()
+        begin = g * group
+        for j in range(HEADS // 4):
+            h = g * (HEADS // 2) + 2 * j
+            even, odd = grads[h, rows:], grads[h + 1, rows:]
+            at = pl.ds(pl.multiple_of(begin + 128 * j, 128), 128)
+            dqkv_s[:half, at] = jnp.where(left_half, even, swap_halves(odd))
+            dqkv_s[half:, at] = jnp.where(left_half, swap_halves(even), odd)
+        for n in range(HEADS // 2):
+            at = pl.ds(pl.multiple_of(begin + 256 + 128 * n, 128), 128)
+            dqkv_s[:, at] = grads[g * (HEADS // 2) + n, :rows]
+
+    def weight_grad(c, n, g):
+        at = pl.multiple_of((2 * n + c) * 128, 128)
+        return mm(a1[:, pl.ds(at, 128)], dqkv_s[:, columns_of(g)], TN).reshape(4, 2, 16, group)
+
+    def over(g):
+        return remote(lanes_of(r.core_ou, r, g), got_q.at[g], r.e_send.at[g], r.e_recv.at[g], to_core)
+
+    parts = []
+    for position, g in enumerate((1 - hz, hz)):
+        enter(g)
+        for n in range(2):
+            lanes_of(r.core_ou, r, g)[n] = weight_grad(oc, n, g).astype(BF16)
+        over(g).start()
+        w = qkv_all[:, :, :, :, :, columns_of(g)].reshape(width, group)
+        part = mm(dqkv_s[:, columns_of(g)], w, NT)
+        if position:
+            r.dh_s[...] += part
+        else:
+            r.dh_s[...] = part
+        for n in range(2):
+            lanes_of(r.acc_ou, r, g)[n] = weight_grad(core, n, g)
+        over(g).wait()
+        acc_q = lanes_of(r.acc_ou, r, g)
+        acc_q[...] = acc_q[...] + got_q[g].astype(F32)
+        parts.append(reducer_of(r, "q", (2 + g) * REDUCE_COPIES, g))
+        parts[-1][0](1)
+
+    columns = jnp.sum(dqkv_s[:, : 3 * width].astype(F32), axis=0, keepdims=True)
+    for j in range(HEADS // 2):
+        at = (j // 2) * group + (j % 2) * 128
+        sums[0:1, 128 * j : 128 * (j + 1)] = columns[:, at : at + 128]
+        at = (j // 2) * group + 256 + (j % 2) * 256
+        pair = jnp.where(
+            left1, swap_halves(columns[:, at : at + 128]), columns[:, at + 128 : at + 256]
+        )
+        sums[0:1, width + 128 * j : width + 128 * (j + 1)] = pair
+    dh = r.dh_s[...]
+    gain = vec[0:1, base : base + width]
+    value = tokens[...].astype(F32)
+    center = jnp.mean(value, axis=1, keepdims=True)
+    offset = value - center
+    spread = jnp.mean(offset * offset, axis=1, keepdims=True)
+    inverse = lax.rsqrt(spread + eps_norm)
+    norm = offset * inverse
+    sums[0:1, base : base + width] = jnp.sum(dh * norm, axis=0, keepdims=True)
+    sums[0:1, base + width : base + 2 * width] = jnp.sum(dh, axis=0, keepdims=True)
+
+    def small_block(a, b, c, d):
+        n = (a * 2 + b) * 8 + c * 2 + d
+        piece = sums[0:1, pl.ds(pl.multiple_of(128 * n, 128), 128)]
+        pair = sums[0:1, pl.ds(pl.multiple_of(base + 128 * (n // 2), 128), 128)]
+        own = pair if d == 0 else swap_halves(pair)
+        return jnp.concatenate([piece, own, jnp.zeros((6, 128), F32)], axis=0)
+
+    for a in range(2):
+        for c in range(4):
+            for d in range(2):
+                core_small[a, c, d] = small_block(a, oc, c, d)
+                acc_small[a, c, d] = small_block(a, core, c, d)
+    over_small = remote(core_small, got_small, r.e_send.at[2], r.e_recv.at[2], to_core)
+    over_small.start()
+    parts[0][1](1)
+    parts[0][0](2)
+    over_small.wait()
+    acc_small[...] += got_small[...]
+    parts.append(reducer_of(r, "small", 4 * REDUCE_COPIES))
+    parts[2][0](1)
+    e = dh * gain
+    mean_e = jnp.mean(e, axis=1, keepdims=True)
+    mean_en = jnp.mean(e * norm, axis=1, keepdims=True)
+    r.grad_tokens[...] = dx[...] + inverse * (e - mean_e - norm * mean_en)
+    parts[1][1](1)
+    parts[1][0](2)
+    parts[0][1](2)
+    parts[0][0](3)
+    parts[2][1](1)
+    parts[2][0](2)
+    parts[1][1](2)
+    parts[1][0](3)
+    parts[2][1](2)
+    parts[2][0](3)
+    for part in (reducer_of(r, "ou", 0), reducer_of(r, "down", REDUCE_COPIES)):
+        part[1](3)
+    r.sum_ou[...] = reducer_of(r, "ou", 0)[2]()
+    r.sum_down[...] = reducer_of(r, "down", REDUCE_COPIES)[2]()
+    for _, finish, _ in parts:
+        finish(3)
+    for g, part in zip((1 - hz, hz), parts):
+        r.sum_qkv[g] = part[2]()
+    r.sum_small[...] = parts[2][2]()
+    for index in range(HEADS):
+        if index:
+            for is_query, count in ((0, rows), (1, half)):
+                view = r.packed.at[0, pl.ds(rows * is_query, count)]
+                pltpu.make_async_copy(view, view, r.b_send.at[index + 8 * is_query]).wait()
+            view = r.o2_s.at[0]
+            pltpu.make_async_copy(view, view, r.d_send.at[index]).wait()
+
+
+def layer_kernel(names, *refs):
+    r = types.SimpleNamespace(**dict(zip(names, refs)))
+    forward_phase(r)
+    middle_phase(r)
+    backward_phase(r)
+    last_phase(r)
+
+
+def layer(inputs, cid):
+    rows, width = inputs["tokens"].shape
+    length = rows * HEADS
+    lanes = 2 * HALF
+    hidden = inputs["up_flat"].shape[0] * 128 // 16
+    down_rows = inputs["down_flat"].shape[0] * 128 // width
+    group = 3 * width // 2
+    every = (2, 2, 4, 2)
+    mine = (2, 4, 2)
+    row = (8, 4096 + 4 * width)
+    vmem = pltpu.VMEM
+    dma = pltpu.SemaphoreType.DMA
+    outputs = {
+        "out_ref": jax.ShapeDtypeStruct((rows, width), BF16),
+        "grad_tokens": jax.ShapeDtypeStruct((rows, width), F32),
+        "sum_qkv": jax.ShapeDtypeStruct((2, 16, group), F32),
+        "sum_ou": jax.ShapeDtypeStruct((16, width + hidden), F32),
+        "sum_down": jax.ShapeDtypeStruct((down_rows, width), F32),
+        "sum_small": jax.ShapeDtypeStruct((8, 128), F32),
+    }
+    scratch = {
+        "a1": vmem((rows, width), BF16),
+        "got": vmem((HEADS, rows + rows // 2, lanes), BF16),
+        "mix": vmem((HEADS, rows // 2, lanes), BF16),
+        "o_heads": vmem((length, lanes), F32),
+        "lse": vmem((8, length), F32),
+        "vec": vmem(row, F32),
+        "qkv_all": vmem(every + (16, 3 * width + 128), BF16),
+        "ou_all": vmem(every + (16, width + hidden), BF16),
+        "down_all": vmem(every + (down_rows, width), BF16),
+        "stage": vmem((256, 128), F32),
+        "qkv_own": vmem((16, 3 * width + 128), BF16),
+        "ou_own": vmem((16, width + hidden), BF16),
+        "down_own": vmem((down_rows, width), BF16),
+        "packed": vmem((HEADS, rows + rows // 2, lanes), BF16),
+        "q_s": vmem((length, lanes), BF16),
+        "k_s": vmem((length, lanes), BF16),
+        "v_s": vmem((length, lanes), BF16),
+        "m_s": vmem((length, lanes), F32),
+        "acc_s": vmem((length, lanes), F32),
+        "o2_s": vmem((HEADS, rows // 2, lanes), BF16),
+        "do2": vmem((HEADS, rows // 2, lanes), BF16),
+        "acc_ou": vmem(mine + (16, width + hidden), F32),
+        "acc_down": vmem(mine + (down_rows, width), F32),
+        "sums": vmem(row, F32),
+        "o_s": vmem((rows, width), BF16),
+        "x1_s": vmem((rows, width), F32),
+        "n2_s": vmem((rows, width), F32),
+        "a2_s": vmem((rows, width), BF16),
+        "gl_s": vmem((rows, hidden), BF16),
+        "du_s": vmem((rows, hidden), BF16),
+        "dh_s": vmem((rows, width), F32),
+        "da_s": vmem((rows, width), BF16),
+        "r_s": vmem((rows, lanes), F32),
+        "core_ou": vmem(mine + (16, width + hidden), BF16),
+        "core_down": vmem(mine + (down_rows, width), BF16),
+        "got_ou": vmem(mine + (16, width + hidden), BF16),
+        "got_down": vmem(mine + (down_rows, width), BF16),
+        "delta_s": vmem((8, length), F32),
+        "grads": vmem((HEADS, rows + rows // 2, lanes), BF16),
+        "got_q": vmem((2,) + mine + (16, group), BF16),
+        "core_small": vmem(mine + (8, 128), F32),
+        "got_small": vmem(mine + (8, 128), F32),
+        "acc_small": vmem(mine + (8, 128), F32),
+    }
+    for name, lead, r, w, wire in (
+        ("ou", (), 16, width + hidden, BF16),
+        ("down", (), down_rows, width, BF16),
+        ("q", (2,), 16, group, BF16),
+        ("small", (), 8, 128, F32),
+    ):
+        for n, buf in enumerate(reduce_buffers(r, w, wire)):
+            scratch[f"{name}{n}"] = vmem(lead + buf.shape, buf.dtype)
+    for name, count in (
+        ("g_own", 3),
+        ("g_send", 33),
+        ("g_recv", 33),
+        ("f_send", 20),
+        ("f_recv", 20),
+        ("x_send", 16),
+        ("x_recv", 16),
+        ("o_send", 8),
+        ("o_recv", 8),
+        ("d_send", 8),
+        ("d_recv", 8),
+        ("c_send", 2),
+        ("c_recv", 2),
+        ("r_send", 5 * REDUCE_COPIES),
+        ("r_recv", 5 * REDUCE_COPIES),
+        ("b_send", 16),
+        ("b_recv", 16),
+        ("e_send", 3),
+        ("e_recv", 3),
+    ):
+        scratch[name] = dma((count,))
+    names = tuple(inputs) + tuple(outputs) + tuple(scratch)
+
+    def kernel(*refs):
+        layer_kernel(names, *refs)
+
+    return pl.pallas_call(
+        kernel,
+        out_shape=list(outputs.values()),
+        in_specs=[SMEM_SPEC if n == "flags" else VMEM_SPEC for n in inputs],
+        out_specs=[VMEM_SPEC] * len(outputs),
+        scratch_shapes=list(scratch.values()),
+        compiler_params=params(cid),
+    )(*inputs.values())
+
+
+def flatten_kernel(sum_qkv, sum_ou, sum_down, sum_small, qkv_o, out_o, up_o, down_o, bias_o, norm_o):
+    groups = sum_down.shape[1] // 128
+    left = left_lanes(16)
+
+    def group(ref, j):
+        return ref[:, 128 * j : 128 * (j + 1)]
+
+    for j in range(groups):
+        part = sum_qkv.at[j // 2]
+        pair = j % 2
+        qkv_o[pl.ds(j, 16, stride=3 * groups), :] = group(part, pair)
+        even, odd = group(part, 2 + 2 * pair), group(part, 3 + 2 * pair)
+        qkv_o[pl.ds(groups + j, 16, stride=3 * groups), :] = jnp.where(
+            left, even, swap_halves(odd)
+        )
+        qkv_o[pl.ds(2 * groups + j, 16, stride=3 * groups), :] = jnp.where(
+            left, swap_halves(even), odd
+        )
+        out_o[pl.ds(j, 16, stride=groups), :] = group(sum_ou, j)
+        down_o[pl.ds(j, sum_down.shape[0], stride=groups), :] = group(sum_down, j)
+    ups = sum_ou.shape[1] // 128 - groups
+    for j in range(ups):
+        up_o[pl.ds(j, 16, stride=ups), :] = group(sum_ou, groups + j)
+    bias_o[...] = sum_small[0:1]
+    norm_o[...] = sum_small[1:2, : norm_o.shape[1]]
+
+
+def flatten(sum_qkv, sum_ou, sum_down, sum_small, norm_len):
+    width = sum_down.shape[1]
+    sizes = (
+        sum_qkv.size // 128,
+        width * 16 // 128,
+        (sum_ou.shape[1] - width) * 16 // 128,
+        sum_down.size // 128,
+    )
+    return pl.pallas_call(
+        flatten_kernel,
+        out_shape=[jax.ShapeDtypeStruct((n, 128), F32) for n in sizes]
+        + [jax.ShapeDtypeStruct((1, 128), F32), jax.ShapeDtypeStruct((1, norm_len), F32)],
+        in_specs=[VMEM_SPEC] * 4,
+        out_specs=[VMEM_SPEC] * 6,
+        compiler_params=params(),
+    )(sum_qkv, sum_ou, sum_down, sum_small)
+
+
+def fast_device(
+    tokens, piece_starts, qkv_weight, out_weight, up_weight, down_weight, biases, norms, cotangent
+):
+    length = tokens.shape[1] * HEADS
+    openings = jnp.arange(length // PIECE, dtype=jnp.int32) * PIECE
+    flags = jnp.any(openings[:, None] == piece_starts[0][None, :], axis=1).astype(jnp.int32)
+    bias_len = biases.shape[0]
+    norm_len = norms.shape[0]
+    small = jnp.concatenate([biases, norms, jnp.zeros((16 * 128 - bias_len - norm_len,), BF16)])
+    output, grad_tokens, sum_qkv, sum_ou, sum_down, sum_small = layer(
+        {
+            "flags": flags,
+            "tokens": tokens[0],
+            "cot": cotangent[0],
+            "small": small.reshape(16, 128),
+            "qkv_flat": qkv_weight.reshape(-1, 128),
+            "out_flat": out_weight.reshape(-1, 128),
+            "up_flat": up_weight.reshape(-1, 128),
+            "down_flat": down_weight.reshape(-1, 128),
+        },
+        1,
+    )
+    flats = flatten(sum_qkv, sum_ou, sum_down, sum_small, norm_len)
+    return (output[None], grad_tokens[None]) + tuple(f.reshape(-1) for f in flats)
+
+
 def solution(mesh):
-    in_specs = (
-        P("dp", "ctx", None),
-        P("dp", None),
-        P(("dp", "ctx")),
-        P(("dp", "ctx")),
-        P(("dp", "ctx")),
-        P(("dp", "ctx")),
-        P(("dp", "ctx")),
-        P(("dp", "ctx")),
-        P("dp", "ctx", None),
-    )
-    out_specs = (
-        P("dp", "ctx", None),
-        P("dp", "ctx", None),
-        P(("dp", "ctx")),
-        P(("dp", "ctx")),
-        P(("dp", "ctx")),
-        P(("dp", "ctx")),
-        P(("dp", "ctx")),
-        P(("dp", "ctx")),
-    )
+    flat = P(("dp", "ctx"))
+    rows = P("dp", "ctx", None)
+    fast = mesh.shape["dp"] == 4 and mesh.shape["ctx"] == HEADS
     return jax.shard_map(
-        per_device, mesh=mesh, in_specs=in_specs, out_specs=out_specs, check_vma=False
-    )
+        fast_device if fast else general_device,
+        mesh=mesh,
+        in_specs=(rows, P("dp", None), flat, flat, flat, flat, flat, flat, rows),
+        out_specs=(rows, rows, flat, flat, flat, flat, flat, flat),
+        check_vma=False,
+    )

time: 1430 us -> 189 us (0.13); the launches traced: 1410 us -> 188 us
  matrix products: 510 us -> 0 us
  waiting for transfers between devices: 290 us -> 0 us
  blocking collectives: 245 us -> 0 us
  Pallas kernels: 0 us -> 182 us
  local copies, waits for them, and re-layouts: 180 us -> 4.82 us
  other arithmetic: 141 us -> 0.61 us
  loops' own time: 33.2 us -> 0 us
    dot_general x124 -> x0, matrix products: 510 us -> none  [the longest x16 91 us: key_terms(): jnp.einsum('hqk,qhd->hkd', dscores, query_block, preferred_element_type=j...]
    pallas_call x0 -> x2, Pallas kernels: none -> 182 us  [the longest x1 180 us: layer(): pl.pallas_call(kernel, out_shape=list(outputs.values()), in_specs=[SMEM_S...]
    unnamed x9 -> x0, waiting for transfers between devices: 178 us -> none
    all_gather x3 -> x0, blocking collectives: 165 us -> none  [the longest x1 68.2 us: per_device(): lax.all_gather(out_weight, ('dp', 'ctx'), axis=0, tiled=True)]
    all_gather x7 -> x0, waiting for transfers between devices: 113 us -> none  [the longest x1 62.1 us: per_device(): lax.all_gather(key_rows, 'ctx', axis=0, tiled=True)]
    unnamed x2 -> x0, blocking collectives: 80.6 us -> none
    reduce_sum x27 -> x0, other arithmetic: 65.4 us -> none  [the longest x16 54.5 us: forward_one_block(): running_sum = running_sum * correction + jnp.sum(exp_scores, axis=-1)]
    dynamic_slice x48 -> x0, local copies, waits for them, and re-layouts: 38.4 us -> none  [forward_compute(): lax.scan(forward_one_block, state, (key_blocks, value_blocks, jnp.arange(...]
  transfers between devices with their start and end apart: 8 -> 0, of which waited for: 3 -> 0; matrix products, arithmetic and copies ran while one was open for 36% -> 0% of each run, Pallas kernels for 0% -> 0%
where the time goes in v2:
time: 189 us; the launch traced here: 188 us
  Pallas kernels  182 us (96%)
  local copies, waits for them, and re-layouts  4.82 us (3%)
    pallas_call x1, Pallas kernels, layer(): pl.pallas_call(kernel, out_shape=list(outputs.values()), in_specs=[SMEM_S...  180 us
    unnamed x10, local copies, waits for them, and re-layouts  4.14 us

profile of v2, /device:TPU:0, one launch (start us, length us, event | category | flops | bytes accessed | tf_op | source)
XLA Modules:
  0.0 188.5 jit_solution(4073126725836916628)
XLA Ops:
  0.6 0.0 copy-start.1
  0.6 0.0 copy-start.2
  0.7 0.6 copy-done.1
  1.3 0.0 copy-done.2
  1.3 0.7 concatenate.3
  2.0 0.0 copy-start.3
  2.0 0.7 copy-done.3
  2.6 0.1 compare_reduce_fusion
  2.7 0.5 convert_element_type.3.refs_0_
  3.2 180.5 %shard_map.152 = (bf16[512,512]{1,0:T(8,128)(2,1)}, f32[512,512]{1,0:T(8,128)}, f32[2,16,768]{2,1,0:T(8,128)}, f32[16,2560]{1,0:T(8,128)}, f32[64,512]{1,0:T(8,128)}, /*index=5*/f32[8,128]{1,0:T(8,128)}) custom-call(s32[16]{0:T(128)} %convert_element_type.3.refs_0_, bf16[512,512]{1,0:T(8,128)(2,1)} %bitcast.17, bf16[512,512]{1,0:T(8,128)(2,1)} %bitcast.18, ...), custom_call_target="tpu_custom_call" | custom-call | tf_op jit(solution)/shard_map/pallas_call | solution.py:1526
  183.7 0.0 copy-start
  183.7 1.9 shard_map.153
  185.6 1.9 copy.19
  187.5 0.0 copy-done
  187.5 1.0 copy.20
  (2 shorter events, 0.0 us)
Async XLA Ops:
  0.6 0.7 copy-start.1
  0.6 0.7 copy-start.2
  2.0 0.7 copy-start.3
  183.7 3.8 %copy-start = (f32[512,512]{1,0:T(8,128)S(1)}, f32[512,512]{1,0:T(8,128)}, u32[]{:S(2)}) copy-start(f32[512,512]{1,0:T(8,128)} %get-tuple-element.21) | copy-start | bytes 3145732

commit v3 on v2

--- a/solution.py
+++ b/solution.py
@@ -623,13 +623,15 @@
     left16 = left_lanes(16)
     for j in range(groups):
         k_pair, v_pair = qkv[groups + j], qkv[2 * groups + j]
-        at = (j // 2) * group + (j % 2) * 128
-        qkv_own[:, at : at + 128] = qkv[j].astype(BF16)
-        at = (j // 2) * group + 256 + (j % 2) * 256
-        qkv_own[:, at : at + 128] = jnp.where(left16, k_pair, swap_halves(v_pair)).astype(BF16)
+        own = qkv_own.at[j // 2]
+        at = (j % 2) * 128
+        own[:, at : at + 128] = qkv[j].astype(BF16)
+        at = 256 + (j % 2) * 256
+        own[:, at : at + 128] = jnp.where(left16, k_pair, swap_halves(v_pair)).astype(BF16)
         at += 128
-        qkv_own[:, at : at + 128] = jnp.where(left16, swap_halves(k_pair), v_pair).astype(BF16)
-    qkv_own[:, 3 * width :] = small[...]
+        own[:, at : at + 128] = jnp.where(left16, swap_halves(k_pair), v_pair).astype(BF16)
+    for g in range(2):
+        qkv_own[g, :, group:] = small[...]
     greet(
         [device(x, core, (z + c) % 4, (y + d) % 2) for c in range(4) for d in range(2)][1:]
         + [to_x, to_core]
@@ -676,43 +678,48 @@
         for copy in phase_copies(phase, a):
             copy.wait()
 
-    first = arrays[0][1]
-
-    def hop(src, dst, peer, n):
-        return remote(src, dst, f_send.at[n], f_recv.at[n], peer)
-
-    def to_xy(c):
-        part = first.at[x, core, c, y]
-        return hop(part, part, to_x, 4 + c), hop(part, part, to_y, 8 + c)
-
-    def corner(c, over_x):
+    hz = z // 2
+
+    def picked(position, half_z):
+        return half_z * (1 - position) + (1 - half_z) * position
+
+    def hop(src, dst, peer, g, n):
+        return remote(src, dst, f_send.at[20 * g + n], f_recv.at[20 * g + n], peer)
+
+    def to_xy(g, c):
+        part = qkv_all.at[g, x, core, c, y]
+        return hop(part, part, to_x, g, 4 + c), hop(part, part, to_y, g, 8 + c)
+
+    def corner(g, c, over_x):
         if over_x:
-            part = first.at[x, core, c, oy]
-            return hop(part, part, to_x, 12 + c)
-        part = first.at[ox, core, c, y]
-        return hop(part, part, to_y, 12 + c)
-
-    def to_sibling(n):
+            part = qkv_all.at[g, x, core, c, oy]
+            return hop(part, part, to_x, g, 12 + c)
+        part = qkv_all.at[g, ox, core, c, y]
+        return hop(part, part, to_y, g, 12 + c)
+
+    def to_sibling(g, n):
         part = (
-            first.at[x, core, :, y],
-            first.at[ox, core, :, y],
-            first.at[x, core, :, oy],
-            first.at[ox, core, :, oy],
+            qkv_all.at[g, x, core, :, y],
+            qkv_all.at[g, ox, core, :, y],
+            qkv_all.at[g, x, core, :, oy],
+            qkv_all.at[g, ox, core, :, oy],
         )[n]
-        return hop(part, part, to_core, 16 + n)
-
-    own_first = pltpu.make_async_copy(qkv_own, first.at[x, core, z, y], g_own.at[0])
+        return hop(part, part, to_core, g, 16 + n)
+
+    def along(g, n):
+        return hop(
+            qkv_own.at[g], qkv_all.at[g, x, core, z, y], device(x, core, others[n], y), g, n
+        )
+
+    own_first = pltpu.make_async_copy(qkv_own, qkv_all.at[:, x, core, z, y], g_own.at[0])
     own_first.start()
-    along = [
-        hop(qkv_own, first.at[x, core, z, y], device(x, core, other, y), n)
-        for n, other in enumerate(others)
-    ]
-    own_xy = [
-        hop(qkv_own, first.at[x, core, z, y], to_x, 4 + z),
-        hop(qkv_own, first.at[x, core, z, y], to_y, 8 + z),
-    ]
-    for copy in along + own_xy:
-        copy.start()
+    for position in range(2):
+        for n, other in enumerate(others):
+            along(picked(position, other // 2), n).start()
+        g = picked(position, hz)
+        own = qkv_all.at[g, x, core, z, y]
+        hop(qkv_own.at[g], own, to_x, g, 4 + z).start()
+        hop(qkv_own.at[g], own, to_y, g, 8 + z).start()
     out_parts = unflatten(out_flat, stage, 16, groups)
     for j in range(groups):
         ou_own[:, 128 * j : 128 * (j + 1)] = out_parts[j].astype(BF16)
@@ -728,41 +735,50 @@
     launch(1, 1)
     launch(1, 2)
     own_first.wait()
-    for n in range(3):
-        along[n].wait_recv()
-        for copy in to_xy((z + 3 - n) % 4):
-            copy.start()
-    to_sibling(0).start()
+    one, two = picked(0, hz), picked(1, hz)
+    for g in (one, two):
+        for n in range(3):
+            along(g, n).wait_recv()
+            for copy in to_xy(g, (z + 3 - n) % 4):
+                copy.start()
+        to_sibling(g, 0).start()
     value = tokens[...].astype(F32)
     center = jnp.mean(value, axis=1, keepdims=True)
     offset = value - center
     spread = jnp.mean(offset * offset, axis=1, keepdims=True)
     norm_s[...] = offset * lax.rsqrt(spread + eps_norm)
-    for c in [z] + others:
-        over_x, over_y = to_xy(c)
-        over_x.wait_recv()
-        over_y.wait_recv()
-
-        @pl.when(c < 2)
-        def _():
-            corner(c, True).start()
-
-        @pl.when(c >= 2)
-        def _():
-            corner(c, False).start()
-
-    to_sibling(1).start()
-    to_sibling(2).start()
-    for c in range(4):
-        corner(c, c < 2).wait()
-    to_sibling(3).start()
-    for n in range(4):
-        to_sibling(n).wait()
-    for copy in along:
-        copy.wait_send()
-    for c in range(4):
-        for copy in to_xy(c):
-            copy.wait_send()
+
+    def meet(g):
+        for c in [z] + others:
+            over_x, over_y = to_xy(g, c)
+            over_x.wait_recv()
+            over_y.wait_recv()
+
+            @pl.when(c < 2)
+            def _():
+                corner(g, c, True).start()
+
+            @pl.when(c >= 2)
+            def _():
+                corner(g, c, False).start()
+
+        to_sibling(g, 1).start()
+        to_sibling(g, 2).start()
+
+    def turn(g):
+        for c in range(4):
+            corner(g, c, c < 2).wait()
+        to_sibling(g, 3).start()
+
+    def close(g):
+        for n in range(4):
+            to_sibling(g, n).wait()
+
+    meet(one)
+    meet(two)
+    turn(one)
+    turn(two)
+    close(one)
 
     vec_ref[...] = jnp.zeros_like(vec_ref)
     devices = [(a, b, c, d) for a in range(2) for b in range(2) for c in range(4) for d in range(2)]
@@ -770,13 +786,13 @@
 
     def bias_rows(begin, end):
         for n in range(begin, end):
-            piece = first[devices[n] + (slice(None), pl.ds(3 * width, 128))].astype(F32)
+            piece = qkv_all[(one,) + devices[n] + (slice(None), pl.ds(group, 128))].astype(F32)
             vec_ref[0:1, 128 * n : 128 * (n + 1)] = piece[0:1]
 
     def norm_rows(begin, end):
         for n in range(begin, end):
             pair = [
-                first[devices[2 * n + d] + (slice(None), pl.ds(3 * width, 128))].astype(F32)
+                qkv_all[(one,) + devices[2 * n + d] + (slice(None), pl.ds(group, 128))].astype(F32)
                 for d in range(2)
             ]
             joined = jnp.concatenate([pair[0][1:2, :HALF], pair[1][1:2, :HALF]], axis=1)
@@ -803,17 +819,24 @@
             else:
                 remote(src, dst, x_send.at[n], x_recv.at[n], device(x, core, tz, ty)).start()
 
-    hz = z // 2
-    order = (hz * 2 + 1 - z % 2, z, (1 - hz) * 2 + z % 2, (1 - hz) * 2 + 1 - z % 2)
+    order = (
+        hz * 2 + 1 - z % 2,
+        z,
+        (1 - hz) * 2 + z % 2,
+        (1 - hz) * 2 + 1 - z % 2,
+    )
     marks = (2, 0, 4, 6)
     left1 = left_lanes(1)
-    for tz, mark in zip(order, marks):
+    for place_of, (tz, mark) in enumerate(zip(order, marks)):
+        if place_of == 2:
+            close(two)
+        g = one if place_of < 2 else two
         a1 = a1_ref[...]
-        at = pl.multiple_of(tz // 2 * group + tz % 2 * 128, 128)
-        w_q = qkv_all[:, :, :, :, :, pl.ds(at, 128)].reshape(width, 128)
+        at = pl.multiple_of(tz % 2 * 128, 128)
+        w_q = qkv_all[g, :, :, :, :, :, pl.ds(at, 128)].reshape(width, 128)
         q = (mm(a1, w_q) + vec_ref[0:1, pl.ds(pl.multiple_of(128 * tz, 128), 128)]).astype(BF16)
-        at_kv = pl.multiple_of(tz // 2 * group + 256 + tz % 2 * 256, 128)
-        w_kv = qkv_all[:, :, :, :, :, pl.ds(at_kv, 256)].reshape(width, 256)
+        at_kv = pl.multiple_of(256 + tz % 2 * 256, 128)
+        w_kv = qkv_all[g, :, :, :, :, :, pl.ds(at_kv, 256)].reshape(width, 256)
         bias = vec_ref[0:1, pl.ds(pl.multiple_of(width + 128 * tz, 128), 128)]
         kv = mm(a1, w_kv)
         even = kv[:, :128] + jnp.where(left1, 0.0, swap_halves(bias))
@@ -836,7 +859,7 @@
         send_all(False)
         pl.when(hz == 0)(lambda: send_all(True))
 
-    pl.when(z % 2 == 0)(send_cross)
+    send_cross()
     finish(1, 1)
     finish(1, 2)
     launch(2, 1)
@@ -879,7 +902,6 @@
 
         @pl.when(n == 3)
         def _():
-            pl.when(z % 2 == 1)(send_cross)
             for a in (1, 2):
                 finish(2, a)
                 launch(3, a)
@@ -948,6 +970,12 @@
     lax.fori_loop(0, 10, step, (queries, keys, ends))
     for a in (1, 2):
         finish(4, a)
+    for g in range(2):
+        for n in range(3):
+            along(g, n).wait_send()
+        for c in range(4):
+            for copy in to_xy(g, c):
+                copy.wait_send()
     for index in range(8):
         block_wait(o_recv, index, mix.at[0])
         if index:
@@ -1231,14 +1259,12 @@
             for n in range(quarter):
                 enter(low * quarter + n)
 
-        for stage, step in ((1, 4), (2, 6)):
-
-            @pl.when(row == step)
-            def _():
-                for _, finish, _ in sums:
-                    finish(stage)
-                for launch, _, _ in sums:
-                    launch(stage + 1)
+        @pl.when(row == 4)
+        def _():
+            for _, finish, _ in sums:
+                finish(1)
+            for launch, _, _ in sums:
+                launch(2)
 
         a_low = own * (3 - i) + (1 - own) * (7 - i)
         a_high = own * (4 + i) + (1 - own) * i
@@ -1326,10 +1352,14 @@
     parts = []
     for position, g in enumerate((1 - hz, hz)):
         enter(g)
+        if position == 0:
+            for early in (reducer_of(r, "ou", 0), reducer_of(r, "down", REDUCE_COPIES)):
+                early[1](2)
+                early[0](3)
         for n in range(2):
             lanes_of(r.core_ou, r, g)[n] = weight_grad(oc, n, g).astype(BF16)
         over(g).start()
-        w = qkv_all[:, :, :, :, :, columns_of(g)].reshape(width, group)
+        w = qkv_all[g, :, :, :, :, :, :group].reshape(width, group)
         part = mm(dqkv_s[:, columns_of(g)], w, NT)
         if position:
             r.dh_s[...] += part
@@ -1450,11 +1480,11 @@
         "o_heads": vmem((length, lanes), F32),
         "lse": vmem((8, length), F32),
         "vec": vmem(row, F32),
-        "qkv_all": vmem(every + (16, 3 * width + 128), BF16),
+        "qkv_all": vmem((2,) + every + (16, group + 128), BF16),
         "ou_all": vmem(every + (16, width + hidden), BF16),
         "down_all": vmem(every + (down_rows, width), BF16),
         "stage": vmem((256, 128), F32),
-        "qkv_own": vmem((16, 3 * width + 128), BF16),
+        "qkv_own": vmem((2, 16, group + 128), BF16),
         "ou_own": vmem((16, width + hidden), BF16),
         "down_own": vmem((down_rows, width), BF16),
         "packed": vmem((HEADS, rows + rows // 2, lanes), BF16),
@@ -1500,8 +1530,8 @@
         ("g_own", 3),
         ("g_send", 33),
         ("g_recv", 33),
-        ("f_send", 20),
-        ("f_recv", 20),
+        ("f_send", 40),
+        ("f_recv", 40),
         ("x_send", 16),
         ("x_recv", 16),
         ("o_send", 8),

time: 189 us -> 175 us (0.926)
  Pallas kernels: 182 us -> 168 us
    pallas_call x1, Pallas kernels: 180 us -> 166 us  [layer(): pl.pallas_call(kernel, out_shape=list(outputs.values()), in_specs=[SMEM_S...]
where the time goes in v3:
time: 175 us; the launch traced here: 174 us
  Pallas kernels  168 us (96%)
  local copies, waits for them, and re-layouts  4.82 us (3%)
    pallas_call x1, Pallas kernels, layer(): pl.pallas_call(kernel, out_shape=list(outputs.values()), in_specs=[SMEM_S...  166 us
    unnamed x10, local copies, waits for them, and re-layouts  4.14 us

profile of v3, /device:TPU:0, one launch (start us, length us, event | category | flops | bytes accessed | tf_op | source)
XLA Modules:
  0.0 174.4 jit_solution(118623126517674144)
XLA Ops:
  0.6 0.0 copy-start.1
  0.6 0.0 copy-start.2
  0.7 0.6 copy-done.1
  1.3 0.0 copy-done.2
  1.3 0.7 concatenate.3
  2.0 0.0 copy-start.3
  2.0 0.7 copy-done.3
  2.6 0.1 compare_reduce_fusion
  2.7 0.5 convert_element_type.3.refs_0_
  3.2 166.4 %shard_map.152 = (bf16[512,512]{1,0:T(8,128)(2,1)}, f32[512,512]{1,0:T(8,128)}, f32[2,16,768]{2,1,0:T(8,128)}, f32[16,2560]{1,0:T(8,128)}, f32[64,512]{1,0:T(8,128)}, /*index=5*/f32[8,128]{1,0:T(8,128)}) custom-call(s32[16]{0:T(128)} %convert_element_type.3.refs_0_, bf16[512,512]{1,0:T(8,128)(2,1)} %bitcast.17, bf16[512,512]{1,0:T(8,128)(2,1)} %bitcast.18, ...), custom_call_target="tpu_custom_call" | custom-call | tf_op jit(solution)/shard_map/pallas_call | solution.py:1556
  169.6 0.0 copy-start
  169.6 1.9 %shard_map.153 = (f32[192,128]{1,0:T(8,128)}, f32[64,128]{1,0:T(8,128)}, f32[256,128]{1,0:T(8,128)}, f32[256,128]{1,0:T(8,128)}, f32[1,128]{1,0:T(1,128)}, /*index=5*/f32[1,64]{1,0:T(1,128)}) custom-call(f32[2,16,768]{2,1,0:T(8,128)} %get-tuple-element.22.sum_qkv, f32[16,2560]{1,0:T(8,128)} %get-tuple-element.23.sum_ou, ...), custom_call_target="tpu_custom_call" | custom-call | tf_op jit(solution)/shard_map/pallas_call | solution.py:1601
  171.5 1.9 %copy.19 = bf16[1,512,512]{2,1,0:T(8,128)(2,1)} copy(bf16[1,512,512]{2,1,0:T(8,128)(2,1)} %bitcast.19) | data formatting | bytes 1048576
  173.4 0.0 copy-done
  173.4 1.0 copy.20
  (2 shorter events, 0.0 us)
Async XLA Ops:
  0.6 0.7 copy-start.1
  0.6 0.7 copy-start.2
  2.0 0.7 copy-start.3
  169.6 3.8 %copy-start = (f32[512,512]{1,0:T(8,128)S(1)}, f32[512,512]{1,0:T(8,128)}, u32[]{:S(2)}) copy-start(f32[512,512]{1,0:T(8,128)} %get-tuple-element.21) | copy-start | bytes 3145732

commit v4 on v3

--- a/solution.py
+++ b/solution.py
@@ -567,7 +567,6 @@
 def forward_phase(r):
     flags = r.flags
     tokens = r.tokens
-    small = r.small
     qkv_flat = r.qkv_flat
     out_flat = r.out_flat
     up_flat = r.up_flat
@@ -630,8 +629,19 @@
         own[:, at : at + 128] = jnp.where(left16, k_pair, swap_halves(v_pair)).astype(BF16)
         at += 128
         own[:, at : at + 128] = jnp.where(left16, swap_halves(k_pair), v_pair).astype(BF16)
+    norm_row = jnp.concatenate(
+        [r.norms[...].astype(F32), jnp.zeros((1, 128 - r.norms.shape[1]), F32)], axis=1
+    )
+    block = jnp.concatenate(
+        [r.biases[...].astype(F32), norm_row, jnp.zeros((14, 128), F32)], axis=0
+    )
     for g in range(2):
-        qkv_own[g, :, group:] = small[...]
+        qkv_own[g, :, group:] = block.astype(BF16)
+    for t in range(flags.shape[0]):
+        found = jnp.int32(0)
+        for j in range(r.starts.shape[1]):
+            found = found + (r.starts[0, j] == t * PIECE).astype(jnp.int32)
+        flags[t] = found
     greet(
         [device(x, core, (z + c) % 4, (y + d) % 2) for c in range(4) for d in range(2)][1:]
         + [to_x, to_core]
@@ -1474,6 +1484,7 @@
         "sum_small": jax.ShapeDtypeStruct((8, 128), F32),
     }
     scratch = {
+        "flags": pltpu.SMEM((length // PIECE,), jnp.int32),
         "a1": vmem((rows, width), BF16),
         "got": vmem((HEADS, rows + rows // 2, lanes), BF16),
         "mix": vmem((HEADS, rows // 2, lanes), BF16),
@@ -1556,14 +1567,31 @@
     return pl.pallas_call(
         kernel,
         out_shape=list(outputs.values()),
-        in_specs=[SMEM_SPEC if n == "flags" else VMEM_SPEC for n in inputs],
+        in_specs=[SMEM_SPEC if n == "starts" else VMEM_SPEC for n in inputs],
         out_specs=[VMEM_SPEC] * len(outputs),
         scratch_shapes=list(scratch.values()),
         compiler_params=params(cid),
     )(*inputs.values())
 
 
-def flatten_kernel(sum_qkv, sum_ou, sum_down, sum_small, qkv_o, out_o, up_o, down_o, bias_o, norm_o):
+def flatten_kernel(
+    output,
+    grad_tokens,
+    sum_qkv,
+    sum_ou,
+    sum_down,
+    sum_small,
+    output_o,
+    tokens_o,
+    qkv_o,
+    out_o,
+    up_o,
+    down_o,
+    bias_o,
+    norm_o,
+):
+    output_o[...] = output[...]
+    tokens_o[...] = grad_tokens[...]
     groups = sum_down.shape[1] // 128
     left = left_lanes(16)
 
@@ -1590,7 +1618,7 @@
     norm_o[...] = sum_small[1:2, : norm_o.shape[1]]
 
 
-def flatten(sum_qkv, sum_ou, sum_down, sum_small, norm_len):
+def flatten(output, grad_tokens, sum_qkv, sum_ou, sum_down, sum_small, norm_len):
     width = sum_down.shape[1]
     sizes = (
         sum_qkv.size // 128,
@@ -1600,29 +1628,28 @@
     )
     return pl.pallas_call(
         flatten_kernel,
-        out_shape=[jax.ShapeDtypeStruct((n, 128), F32) for n in sizes]
+        out_shape=[
+            jax.ShapeDtypeStruct(output.shape, output.dtype),
+            jax.ShapeDtypeStruct(grad_tokens.shape, grad_tokens.dtype),
+        ]
+        + [jax.ShapeDtypeStruct((n, 128), F32) for n in sizes]
         + [jax.ShapeDtypeStruct((1, 128), F32), jax.ShapeDtypeStruct((1, norm_len), F32)],
-        in_specs=[VMEM_SPEC] * 4,
-        out_specs=[VMEM_SPEC] * 6,
+        in_specs=[VMEM_SPEC] * 6,
+        out_specs=[VMEM_SPEC] * 8,
         compiler_params=params(),
-    )(sum_qkv, sum_ou, sum_down, sum_small)
+    )(output, grad_tokens, sum_qkv, sum_ou, sum_down, sum_small)
 
 
 def fast_device(
     tokens, piece_starts, qkv_weight, out_weight, up_weight, down_weight, biases, norms, cotangent
 ):
-    length = tokens.shape[1] * HEADS
-    openings = jnp.arange(length // PIECE, dtype=jnp.int32) * PIECE
-    flags = jnp.any(openings[:, None] == piece_starts[0][None, :], axis=1).astype(jnp.int32)
-    bias_len = biases.shape[0]
-    norm_len = norms.shape[0]
-    small = jnp.concatenate([biases, norms, jnp.zeros((16 * 128 - bias_len - norm_len,), BF16)])
     output, grad_tokens, sum_qkv, sum_ou, sum_down, sum_small = layer(
         {
-            "flags": flags,
+            "starts": piece_starts,
             "tokens": tokens[0],
             "cot": cotangent[0],
-            "small": small.reshape(16, 128),
+            "biases": biases.reshape(1, -1),
+            "norms": norms.reshape(1, -1),
             "qkv_flat": qkv_weight.reshape(-1, 128),
             "out_flat": out_weight.reshape(-1, 128),
             "up_flat": up_weight.reshape(-1, 128),
@@ -1630,7 +1657,9 @@
         },
         1,
     )
-    flats = flatten(sum_qkv, sum_ou, sum_down, sum_small, norm_len)
+    output, grad_tokens, *flats = flatten(
+        output, grad_tokens, sum_qkv, sum_ou, sum_down, sum_small, norms.shape[0]
+    )
     return (output[None], grad_tokens[None]) + tuple(f.reshape(-1) for f in flats)
 
 

time: 175 us -> 170 us (0.971)
  local copies, waits for them, and re-layouts: 4.82 us -> 0 us
    unnamed x10 -> x0, local copies, waits for them, and re-layouts: 4.14 us -> none
where the time goes in v4:
time: 170 us
  Pallas kernels  169 us (99%)
    pallas_call x1, Pallas kernels, layer(): pl.pallas_call(kernel, out_shape=list(outputs.values()), in_specs=[SMEM_S...  167 us

profile of v4, /device:TPU:0, one launch (start us, length us, event | category | flops | bytes accessed | tf_op | source)
XLA Modules:
  0.0 170.1 jit_solution(10842924171702711335)
XLA Ops:
  0.6 166.5 %shard_map.152 = (bf16[512,512]{1,0:T(8,128)(2,1)}, f32[512,512]{1,0:T(8,128)}, f32[2,16,768]{2,1,0:T(8,128)}, f32[16,2560]{1,0:T(8,128)}, f32[64,512]{1,0:T(8,128)}, /*index=5*/f32[8,128]{1,0:T(8,128)}) custom-call(s32[1,4]{1,0:T(1,128)} %refs_0_.1, bf16[512,512]{1,0:T(8,128)(2,1)} %bitcast.16, bf16[512,512]{1,0:T(8,128)(2,1)} %bitcast.17, ...), custom_call_target="tpu_custom_call" | custom-call | tf_op jit(solution)/shard_map/pallas_call | solution.py:1567
  167.2 2.8 %shard_map.153 = (bf16[512,512]{1,0:T(8,128)(2,1)}, f32[512,512]{1,0:T(8,128)}, f32[192,128]{1,0:T(8,128)}, f32[64,128]{1,0:T(8,128)}, f32[256,128]{1,0:T(8,128)...) custom-call(bf16[512,512]{1,0:T(8,128)(2,1)} %get-tuple-element.22.output, ...), custom_call_target="tpu_custom_call" | custom-call | tf_op jit(solution)/shard_map/pallas_call | solution.py:1629

commit v5 on v4

--- a/solution.py
+++ b/solution.py
@@ -1057,7 +1057,7 @@
     a2_s[...] = (n2 * gain + shift).astype(BF16)
     sums_ref[...] = jnp.zeros_like(sums_ref)
 
-    @pl.loop(0, hidden // width)
+    @pl.loop(0, hidden // width, unroll=True)
     def _(j):
         at = pl.multiple_of(j * width, width)
         w_up = ou_all[:, :, :, :, :, pl.ds(pl.multiple_of(width + at, width), width)].reshape(
@@ -1104,8 +1104,8 @@
         send2[2 * j] = jnp.where(left_half, top, swap_halves(low))
         send2[2 * j + 1] = jnp.where(left_half, swap_halves(top), low)
     hz = z // 2
-    order = ((1 - hz) * 2 + z % 2, (1 - hz) * 2 + 1 - z % 2, hz * 2 + 1 - z % 2, z)
-    for tz, mark in zip(order, (4, 6, 2, 0)):
+    order = (hz * 2 + 1 - z % 2, z, (1 - hz) * 2 + z % 2, (1 - hz) * 2 + 1 - z % 2)
+    for tz, mark in zip(order, (2, 0, 4, 6)):
         for step in range(2):
             ty = (y + step) % 2
             index = mark + step
@@ -1264,12 +1264,7 @@
         own = first + last
         i = (row + 3) % 4 + last - 3 * first
 
-        @pl.when(row == 1)
-        def _():
-            for n in range(quarter):
-                enter(low * quarter + n)
-
-        @pl.when(row == 4)
+        @pl.when(row == 6)
         def _():
             for _, finish, _ in sums:
                 finish(1)
@@ -1280,6 +1275,11 @@
         a_high = own * (4 + i) + (1 - own) * i
         a = low * a_low + hz * a_high
         count = own * (3 - i) + cross * i + square * 4
+
+        @pl.when(cross == 1)
+        def _():
+            enter(a)
+
 
         @pl.when(square == 0)
         def _():

time: 170 us -> 163 us (0.959)
  Pallas kernels: 169 us -> 162 us
    pallas_call x1, Pallas kernels: 167 us -> 160 us  [layer(): pl.pallas_call(kernel, out_shape=list(outputs.values()), in_specs=[SMEM_S...]
where the time goes in v5:
time: 163 us
  Pallas kernels  162 us (99%)
    pallas_call x1, Pallas kernels, layer(): pl.pallas_call(kernel, out_shape=list(outputs.values()), in_specs=[SMEM_S...  160 us

profile of v5, /device:TPU:0, one launch (start us, length us, event | category | flops | bytes accessed | tf_op | source)
XLA Modules:
  0.0 163.3 jit_solution(11099963121929299030)
XLA Ops:
  0.6 159.7 %shard_map.152 = (bf16[512,512]{1,0:T(8,128)(2,1)}, f32[512,512]{1,0:T(8,128)}, f32[2,16,768]{2,1,0:T(8,128)}, f32[16,2560]{1,0:T(8,128)}, f32[64,512]{1,0:T(8,128)}, /*index=5*/f32[8,128]{1,0:T(8,128)}) custom-call(s32[1,4]{1,0:T(1,128)} %refs_0_.1, bf16[512,512]{1,0:T(8,128)(2,1)} %bitcast.16, bf16[512,512]{1,0:T(8,128)(2,1)} %bitcast.17, ...), custom_call_target="tpu_custom_call" | custom-call | tf_op jit(solution)/shard_map/pallas_call | solution.py:1567
  160.3 2.8 %shard_map.153 = (bf16[512,512]{1,0:T(8,128)(2,1)}, f32[512,512]{1,0:T(8,128)}, f32[192,128]{1,0:T(8,128)}, f32[64,128]{1,0:T(8,128)}, f32[256,128]{1,0:T(8,128)...) custom-call(bf16[512,512]{1,0:T(8,128)(2,1)} %get-tuple-element.22.output, ...), custom_call_target="tpu_custom_call" | custom-call | tf_op jit(solution)/shard_map/pallas_call | solution.py:1629

commit v6 on v5

--- a/solution.py
+++ b/solution.py
@@ -1264,7 +1264,7 @@
         own = first + last
         i = (row + 3) % 4 + last - 3 * first
 
-        @pl.when(row == 6)
+        @pl.when(row == 8)
         def _():
             for _, finish, _ in sums:
                 finish(1)

time: 163 us -> 164 us (level)
  no operation moved by 1% of the time
where the time goes in v6:
time: 164 us
  Pallas kernels  163 us (99%)
    pallas_call x1, Pallas kernels, layer(): pl.pallas_call(kernel, out_shape=list(outputs.values()), in_specs=[SMEM_S...  160 us

profile of v6, /device:TPU:0, one launch (start us, length us, event | category | flops | bytes accessed | tf_op | source)
XLA Modules:
  0.0 163.6 jit_solution(11258056998906307767)
XLA Ops:
  0.6 160.0 %shard_map.152 = (bf16[512,512]{1,0:T(8,128)(2,1)}, f32[512,512]{1,0:T(8,128)}, f32[2,16,768]{2,1,0:T(8,128)}, f32[16,2560]{1,0:T(8,128)}, f32[64,512]{1,0:T(8,128)}, /*index=5*/f32[8,128]{1,0:T(8,128)}) custom-call(s32[1,4]{1,0:T(1,128)} %refs_0_.1, bf16[512,512]{1,0:T(8,128)(2,1)} %bitcast.16, bf16[512,512]{1,0:T(8,128)(2,1)} %bitcast.17, ...), custom_call_target="tpu_custom_call" | custom-call | tf_op jit(solution)/shard_map/pallas_call | solution.py:1567
  160.7 2.8 %shard_map.153 = (bf16[512,512]{1,0:T(8,128)(2,1)}, f32[512,512]{1,0:T(8,128)}, f32[192,128]{1,0:T(8,128)}, f32[64,128]{1,0:T(8,128)}, f32[256,128]{1,0:T(8,128)...) custom-call(bf16[512,512]{1,0:T(8,128)(2,1)} %get-tuple-element.22.output, ...), custom_call_target="tpu_custom_call" | custom-call | tf_op jit(solution)/shard_map/pallas_call | solution.py:1629
